TPU v7x, 512 devices: a whole 4x4x16 slice. The times are simulated.
512 devices in a mesh: pts: 128 (over x, z, core), help: 4 (over y).
Axes of the slice: x: 4, y: 4, z: 16, core: 2. Of those that a mesh axis runs over, the one named last changes fastest.
Arguments:
- src_points: bfloat16 [131072, 256], P(('pts', 'help')), may hold values from -8 to 8
- dst_points: bfloat16 [131072, 256], P(('pts', 'help')), may hold values from -8 to 8
- src_logw: float32 [131072], P(('pts', 'help')), may hold values from -1.2 to 1.2
- dst_logw: float32 [131072], P(('pts', 'help')), may hold values from -1.2 to 1.2
- init_g: float32 [131072], P(('pts', 'help')), may hold values from -2 to 7000
- pair_lists: int32 [512, 24], P(('pts', 'help')), may hold values from 0 to 511, as said below
- pair_counts: int32 [512], P(('pts', 'help')), may hold values from 3 to 24, as said below
Outputs:
- dual_f: float32 [131072], P(('pts', 'help'))
- dual_g: float32 [131072], P(('pts', 'help'))
Inputs may be any that keep to these rules, and one draw needn't show every extreme that they name: `pair_lists`: row block r's first pair_counts[r] entries are distinct, one of them is r itself, and each names a block whose points are held by an index of pts at most 3 away from the index that holds r; the later entries equal r. `pair_counts`: 24 is reached by some row block in every draw. The counts of the blocks held by one index of pts sum to at most 14 times the number of help devices; dealt out in turn to the help devices of that index, they give some device exactly 24 in every draw.
All inputs are finite; a program needn't handle non-finite values.
Results may differ from a plain program's by a relative error of at most 0.0003.
Values may be sent and summed in bfloat16 or wider, within the bound.
A program may use at most 64 MiB of HBM per device.

v0:
```python
import jax
import jax.numpy as jnp
from jax import lax
from jax.sharding import PartitionSpec as P

PAIR_MOST = 24
REACH = 3
ITERS = 2


EPS = 0.25
NEGATIVE = -1e30


def from_everyone(array, axis):
    peers = lax.axis_size(axis)
    return lax.all_to_all(
        jnp.broadcast_to(array[None], (peers, *array.shape)), axis, 0, 0, tiled=True
    )


def in_order(tiles, dim):
    shape = list(tiles.shape[1:])
    shape[dim] *= tiles.shape[0]
    return jnp.moveaxis(tiles, 0, dim).reshape(shape)


def collect(array, axis, dim):
    tiles = from_everyone(array, axis)
    return in_order(tiles, dim)


def rows_first(arrays, axis, dims):
    turned = [jnp.moveaxis(a, dim, 0) for a, dim in zip(arrays, dims)]
    widths = [t[0].size for t in turned]
    both = jnp.concatenate([t.reshape(-1, w) for t, w in zip(turned, widths)], axis=1)
    result = lax.all_gather(both, axis, axis=0, tiled=True)
    tiles = jnp.split(result, [sum(widths[:k]) for k in range(1, len(widths))], axis=1)
    return tuple(
        (
            jnp.moveaxis(b.reshape(-1, *t.shape[1:]), 0, dim)
            for b, t, dim in zip(tiles, turned, dims)
        )
    )


def shifted(block, axis, distance):
    devices = range(lax.axis_size(axis))
    route = [(i - distance, i) for i in devices if i - distance in devices]
    return lax.ppermute(block, axis, route)


def all_in_one(array, axis):
    leaves = jax.tree.leaves(array)
    order = sorted(range(len(leaves)), key=lambda k: -leaves[k].size)
    width = (1, *leaves[order[0]].shape)[-1]
    lines = [
        jnp.pad(leaves[k].reshape(-1), (0, -leaves[k].size % width)).reshape(-1, width)
        for k in order
    ]
    both, at, found = (from_everyone(jnp.concatenate(lines), axis), 0, {})
    for k, line in zip(order, lines):
        share = both[:, at : at + len(line)].reshape(len(both), -1)
        found[k] = share[:, : leaves[k].size].reshape(-1, *leaves[k].shape)
        at += len(line)
    numbers = iter(range(len(leaves)))
    return jax.tree.map(lambda _: found[next(numbers)], array)


def combined_pairwise(pieces, combine):
    while len(jax.tree.leaves(pieces)[0]) > 1:
        pieces = jax.vmap(combine)(
            *(jax.tree.map(lambda part: part[side::2], pieces) for side in (0, 1))
        )
    return jax.tree.map(lambda part: part[0], pieces)


def merged(array, axis, combine):
    pieces = all_in_one(array, axis)
    return combined_pairwise(pieces, combine)


def merge_pair(earlier, later):
    peak = jnp.maximum(earlier[0], later[0])
    summed = earlier[1] * jnp.exp(earlier[0] - peak) + later[1] * jnp.exp(later[0] - peak)
    return (peak, summed)


def fold_into(tables, position, incoming):
    old_top = lax.dynamic_index_in_dim(tables[0], position, 0, keepdims=False)
    old_sum = lax.dynamic_index_in_dim(tables[1], position, 0, keepdims=False)
    new_top, new_sum = merge_pair((old_top, old_sum), incoming)
    return (
        lax.dynamic_update_index_in_dim(tables[0], new_top, position, 0),
        lax.dynamic_update_index_in_dim(tables[1], new_sum, position, 0),
    )


def pick_two(table, index_pair):
    return [
        lax.dynamic_index_in_dim(table, index_pair[member], 0, keepdims=False)
        for member in range(2)
    ]


def on_device(src_points, dst_points, src_logw, dst_logw, init_g, pair_lists, pair_counts):
    helpers = lax.axis_size("help")
    pts_total = lax.axis_size("pts")
    pts_here = lax.axis_index("pts")
    helper_here = lax.axis_index("help")
    block_rows = src_points.shape[0]
    spot_count = (2 * REACH + 1) * helpers
    offsets = list(range(-REACH, REACH + 1))
    far_offsets = [offset for offset in offsets if offset != 0]
    group_pts = collect(dst_points, "help", 0)
    group_lw, group_g = rows_first((dst_logw, init_g), "help", (0, 0))
    nearby = {0: (group_pts, group_lw, group_g)}
    for heading in (1, -1):
        filled = 1
        while filled < REACH + 1:
            amount = min(filled, REACH + 1 - filled)
            picked = [nearby[-heading * member] for member in range(amount)]
            stacked_pts = jnp.stack([entry[0] for entry in picked])
            stacked_lw = jnp.stack([entry[1] for entry in picked])
            stacked_g = jnp.stack([entry[2] for entry in picked])
            arrived_pts = shifted(stacked_pts, "pts", heading * filled)
            arrived_vals = shifted((stacked_lw, stacked_g), "pts", heading * filled)
            for member in range(amount):
                nearby[-heading * (member + filled)] = (
                    arrived_pts[member],
                    arrived_vals[0][member],
                    arrived_vals[1][member],
                )
            filled += amount
    near_pts = jnp.concatenate([nearby[offset][0] for offset in offsets]).reshape(
        spot_count, block_rows, -1
    )
    near_lw = jnp.concatenate([nearby[offset][1] for offset in offsets]).reshape(
        spot_count, block_rows
    )
    potential = jnp.concatenate([nearby[offset][2] for offset in offsets]).reshape(
        spot_count, block_rows
    )
    near_half = 0.5 * jnp.sum(jnp.square(near_pts.astype(jnp.float32)), axis=2)
    row_pts = src_points[None]
    row_lw = src_logw[None]
    columns = pair_lists[0]
    active = jnp.arange(PAIR_MOST, dtype=jnp.int32) < pair_counts[0]
    row_slot = jnp.zeros((PAIR_MOST,), jnp.int32)
    spots = (columns // helpers - pts_here + REACH) * helpers + columns % helpers
    spots = jnp.clip(spots, 0, spot_count - 1)
    row_half = 0.5 * jnp.sum(jnp.square(row_pts.astype(jnp.float32)), axis=2)
    row_count = row_pts.shape[0]
    pair_total = columns.shape[0] // 2
    pair_spots = spots.reshape(pair_total, 2)
    pair_rows = row_slot.reshape(pair_total, 2)
    pair_active = active.reshape(pair_total, 2)

    def inner_tile(spot_pair, row_pair):
        lefts = pick_two(row_pts, row_pair)
        rights = pick_two(near_pts, spot_pair)
        return jnp.stack(
            [
                lax.dot_general(
                    lefts[member],
                    rights[member],
                    (((1,), (1,)), ((), ())),
                    preferred_element_type=jnp.float32,
                )
                for member in range(2)
            ]
        )

    def cost_of(inner_dot, spot_pair, row_pair):
        return (
            jnp.stack(pick_two(row_half, row_pair))[:, :, None]
            + jnp.stack(pick_two(near_half, spot_pair))[:, None, :]
            - inner_dot
        )

    source_pot = jnp.zeros((row_count, block_rows), jnp.float32)
    group_pot = jnp.zeros((helpers, block_rows), jnp.float32)
    for sweep_index in range(ITERS):
        target_pot = potential

        def row_step(carry, item):
            spot_pair, row_pair, active_pair = item
            inner_dot = inner_tile(spot_pair, row_pair)
            cost_tile = cost_of(inner_dot, spot_pair, row_pair)
            scores = (
                jnp.stack(pick_two(near_lw, spot_pair))[:, None, :]
                + (jnp.stack(pick_two(target_pot, spot_pair))[:, None, :] - cost_tile) / EPS
            )
            tile_top = jnp.max(scores, axis=2)
            tile_sum = jnp.sum(jnp.exp(scores - tile_top[:, :, None]), axis=2)
            tile_top = jnp.where(active_pair[:, None], tile_top, NEGATIVE)
            tile_sum = jnp.where(active_pair[:, None], tile_sum, 0.0)
            for member in range(2):
                carry = fold_into(carry, row_pair[member], (tile_top[member], tile_sum[member]))
            return (carry, None)

        row_initial = (
            jnp.full((row_count, block_rows), NEGATIVE, jnp.float32),
            jnp.zeros((row_count, block_rows), jnp.float32),
        )
        (row_top, row_sum), stored = lax.scan(
            row_step, row_initial, (pair_spots, pair_rows, pair_active)
        )
        source_pot = -EPS * (row_top + jnp.log(row_sum))

        def column_step(carry, item):
            spot_pair, row_pair, active_pair, kept = item
            inner_dot = inner_tile(spot_pair, row_pair)
            cost_tile = cost_of(inner_dot, spot_pair, row_pair)
            scores = (
                jnp.stack(pick_two(row_lw, row_pair))[:, :, None]
                + (jnp.stack(pick_two(source_pot, row_pair))[:, :, None] - cost_tile) / EPS
            )
            tile_top = jnp.max(scores, axis=1)
            tile_sum = jnp.sum(jnp.exp(scores - tile_top[:, None, :]), axis=1)
            tile_top = jnp.where(active_pair[:, None], tile_top, NEGATIVE)
            tile_sum = jnp.where(active_pair[:, None], tile_sum, 0.0)
            for member in range(2):
                carry = fold_into(carry, spot_pair[member], (tile_top[member], tile_sum[member]))
            return (carry, None)

        initial = (
            jnp.full((spot_count, block_rows), NEGATIVE, jnp.float32),
            jnp.zeros((spot_count, block_rows), jnp.float32),
        )
        result, unused = lax.scan(
            column_step, initial, (pair_spots, pair_rows, pair_active, stored)
        )
        col_top, col_sum = result
        slab_top = col_top.reshape(2 * REACH + 1, helpers, block_rows)
        slab_sum = col_sum.reshape(2 * REACH + 1, helpers, block_rows)
        gathered = (slab_top[REACH], slab_sum[REACH])
        for offset in far_offsets:
            arrived = shifted((slab_top[offset + REACH], slab_sum[offset + REACH]), "pts", offset)
            sender = pts_here - offset
            present = (sender >= 0) & (sender < pts_total)
            gathered = merge_pair(
                gathered,
                (jnp.where(present, arrived[0], NEGATIVE), jnp.where(present, arrived[1], 0.0)),
            )
        merged_top, merged_sum = merged((gathered[0], gathered[1]), "help", merge_pair)
        group_pot = -EPS * (merged_top + jnp.log(merged_sum))
        if sweep_index + 1 < ITERS:
            flat_pot = group_pot.reshape(-1)
            pieces = {0: flat_pot}
            for offset in far_offsets:
                pieces[offset] = shifted(flat_pot, "pts", -offset)
            potential = jnp.concatenate([pieces[offset] for offset in offsets]).reshape(
                spot_count, block_rows
            )
    own_f = source_pot[0]
    own_g = lax.dynamic_index_in_dim(group_pot, helper_here, 0, keepdims=False)
    return (own_f, own_g)


def solution(mesh):
    placed = (
        P(("pts", "help"), None),
        P(("pts", "help"), None),
        P(("pts", "help")),
        P(("pts", "help")),
        P(("pts", "help")),
        P(("pts", "help"), None),
        P(("pts", "help")),
    )
    return jax.shard_map(
        on_device,
        mesh=mesh,
        in_specs=placed,
        out_specs=(P(("pts", "help")), P(("pts", "help"))),
        check_vma=False,
    )
```

profile of v0, /device:TPU:7, one launch (start us, length us, event | category | flops | bytes accessed | tf_op | source)
XLA Modules:
  0.0 606.4 jit_solution(11721670042160361558)
XLA Ops:
  1.6 12.6 %all_to_all.15 = bf16[4,256,256]{2,1,0:T(8,128)(2,1)S(1)} all-to-all(bf16[4,256,256]{2,1,0:T(8,128)(2,1)S(1)} %broadcast_in_dim.200), channel_id=1, replica_groups=mesh['pts'=128,'help'=4] {'help'}, dimensions={0} | all-to-all | bytes 1048576 | tf_op jit(solution)/shard_map/all_to_all | solution.py:17
  22.1 8.1 %all_gather.3 = f32[1024,2]{0,1:T(2,128)S(1)} all-gather(f32[256,2]{0,1:T(2,128)S(1)} %pad_maximum_fusion.16), channel_id=1, replica_groups=mesh['pts'=128,'help'=4] {'help'}, dimensions={0}, use_global_device_ids=true | all-gather | bytes 10240 | tf_op jit(solution)/shard_map/all_gather | solution.py:37
  30.2 4.7 collective-permute-start
  34.9 8.0 %collective-permute-start.2 = (f32[1,1024]{1,0:T(1,128)S(1)}, f32[1,1024]{1,0:T(1,128)S(1)}, u32[]{:S(2)}, u32[]{:S(2)}) collective-permute-start(f32[1,1024]{1,0:T(1,128)S(1)} %get-tuple-element.875), channel_id=1, source_target_pairs={{4,0},{8,4},{12,8},{16,12},{20,16},{24,20},{28,24},{32,28},{36,32}... | collective-permute-start | bytes 12296 | tf_op jit(solution)/shard_map/ppermute | solution.py:50
  48.5 5.8 collective-permute-start.6
  59.5 5.5 collective-permute-start.3
  68.7 5.5 collective-permute-start.7
  75.5 5.2 collective-permute-done.1
  81.1 5.7 collective-permute-start.11
  89.2 19.6 %collective-permute-done.11 = bf16[2,1024,256]{2,1,0:T(8,128)(2,1)S(1)} collective-permute-done((bf16[2,1024,256]{2,1,0:T(8,128)(2,1)S(1)}, bf16[2,1024,256]{2,1,0:T(8,128)(2,1)S(1)}, u32[]{:S(2)}, u32[]{:S(2)}) %collective-permute-start.11) | collective-permute-done | bytes 1048608 | tf_op jit(solution)/shard_map/ppermute | solution.py:50
  111.8 91.9 %while.60 = (s32[]{:T(128)}, f32[1,256]{1,0:T(1,128)S(1)}, f32[1,256]{1,0:T(1,128)S(1)}, pred[12,2]{1,0:T(8,128)(4,1)S(1)}, s32[12,2]{0,1:T(2,128)S(1)}, /*index...) while((s32[]{:T(128)}, f32[1,256]{1,0:T(1,128)S(1)}, ...), condition=%wide.region_5.6_spmd.clone, body=%wide.region_2.5_spmd.clone.sunk | while | flops 69080064 | bytes 2160921 | solution.py:206
  203.8 94.4 %while.58 = (s32[]{:T(128)}, f32[28,256]{1,0:T(8,128)S(1)}, f32[28,256]{1,0:T(8,128)S(1)}, s32[12,2]{0,1:T(2,128)S(1)}, pred[12,2]{1,0:T(8,128)(4,1)S(1)}, /*ind...) while((s32[]{:T(128)}, f32[28,256]{1,0:T(8,128)S(1)}, ...), condition=%wide.region_9.10_spmd, body=%wide.region_6.9_spmd.sunk | while | flops 69078536 | bytes 2156831 | solution.py:231
  298.2 7.5 %collective-permute-start.12 = (f32[4,256]{1,0:T(4,128)S(1)}, f32[4,256]{1,0:T(4,128)S(1)}, u32[]{:S(2)}, u32[]{:S(2)}) collective-permute-start(f32[4,256]{1,0:T(4,128)S(1)} %get-tuple-element.860), channel_id=1, source_target_pairs={{12,0},{16,4},{20,8},{24,12},{28,16},{32,20},{36,24},{40,28},{44,3... | collective-permute-start | bytes 12296 | tf_op jit(solution)/shard_map/ppermute | solution.py:50
  318.6 5.8 collective-permute-start.18
  338.5 3.8 collective-permute-done.23
  342.4 7.5 %all_to_all.16 = f32[4,8,256]{2,1,0:T(8,128)S(1)} all-to-all(f32[4,8,256]{2,1,0:T(8,128)S(1)} %broadcast_in_dim.204), channel_id=1, replica_groups=mesh['pts'=128,'help'=4] {'help'}, dimensions={0} | all-to-all | bytes 65536 | tf_op jit(solution)/shard_map/all_to_all | solution.py:17
  354.0 4.5 collective-permute-start.26
  360.9 5.4 collective-permute-start.28
  372.2 90.3 %while.61 = (s32[]{:T(128)}, f32[1,256]{1,0:T(1,128)S(1)}, f32[1,256]{1,0:T(1,128)S(1)}, pred[12,2]{1,0:T(8,128)(4,1)S(1)}, s32[12,2]{0,1:T(2,128)S(1)}, /*index...) while((s32[]{:T(128)}, f32[1,256]{1,0:T(1,128)S(1)}, ...), condition=%wide.region_13.14_spmd.clone, body=%wide.region_10.13_spmd.clone.sunk | while | flops 69080064 | bytes 2160921 | solution.py:206
  463.1 92.2 %while.59 = (s32[]{:T(128)}, f32[28,256]{1,0:T(8,128)S(1)}, f32[28,256]{1,0:T(8,128)S(1)}, s32[12,2]{0,1:T(2,128)S(1)}, pred[12,2]{1,0:T(8,128)(4,1)S(1)}, /*ind...) while((s32[]{:T(128)}, f32[28,256]{1,0:T(8,128)S(1)}, ...), condition=%wide.region_17.18_spmd, body=%wide.region_14.17_spmd.sunk | while | flops 69078536 | bytes 2156831 | solution.py:231
  555.3 4.7 collective-permute-start.30
  573.8 5.5 collective-permute-start.36
  593.6 3.9 collective-permute-done.41
  601.5 4.3 all-to-all-done.2
  (886 shorter events, 279.6 us)
Async XLA Ops:
  14.2 34.2 %collective-permute-start.10 = (bf16[1,1024,256]{2,1,0:T(8,128)(2,1)S(1)}, bf16[1,1024,256]{2,1,0:T(8,128)(2,1)S(1)}, u32[]{:S(2)}, u32[]{:S(2)}) collective-permute-start(bf16[1,1024,256]{2,1,0:T(8,128)(2,1)S(1)} %bitcast.205), channel_id=1, source_target_pairs={{4,0},{8,4},{12,8},{16,12},{20,16},{24,20},{28,24},{32,28},{36,32}... | collective-permute-start | bytes 1572872 | tf_op jit(solution)/shard_map/ppermute | solution.py:50
  17.9 36.3 %collective-permute-start.8 = (bf16[1,1024,256]{2,1,0:T(8,128)(2,1)S(1)}, bf16[1,1024,256]{2,1,0:T(8,128)(2,1)S(1)}, u32[]{:S(2)}, u32[]{:S(2)}) collective-permute-start(bf16[1,1024,256]{2,1,0:T(8,128)(2,1)S(1)} %bitcast.206), channel_id=1, source_target_pairs={{0,4},{4,8},{8,12},{12,16},{16,20},{20,24},{24,28},{28,32},{32,36}... | collective-permute-start | bytes 1572872 | tf_op jit(solution)/shard_map/ppermute | solution.py:50
  30.2 27.3 %collective-permute-start = (f32[1,1024]{1,0:T(1,128)S(1)}, f32[1,1024]{1,0:T(1,128)S(1)}, u32[]{:S(2)}, u32[]{:S(2)}) collective-permute-start(f32[1,1024]{1,0:T(1,128)S(1)} %get-tuple-element.875), channel_id=1, source_target_pairs={{0,4},{4,8},{8,12},{12,16},{16,20},{20,24},{24,28},{28,32},{32,36}... | collective-permute-start | bytes 12296 | tf_op jit(solution)/shard_map/ppermute | solution.py:50
  34.9 22.6 %collective-permute-start.2 = (f32[1,1024]{1,0:T(1,128)S(1)}, f32[1,1024]{1,0:T(1,128)S(1)}, u32[]{:S(2)}, u32[]{:S(2)}) collective-permute-start(f32[1,1024]{1,0:T(1,128)S(1)} %get-tuple-element.875), channel_id=1, source_target_pairs={{4,0},{8,4},{12,8},{16,12},{20,16},{24,20},{28,24},{32,28},{36,32}... | collective-permute-start | bytes 12296 | tf_op jit(solution)/shard_map/ppermute | solution.py:50
  42.9 22.0 %collective-permute-start.4 = (f32[1,1024]{1,0:T(1,128)S(1)}, f32[1,1024]{1,0:T(1,128)S(1)}, u32[]{:S(2)}, u32[]{:S(2)}) collective-permute-start(f32[1,1024]{1,0:T(1,128)S(1)} %get-tuple-element.874), channel_id=1, source_target_pairs={{0,4},{4,8},{8,12},{12,16},{16,20},{20,24},{24,28},{28,32},{32,36}... | collective-permute-start | bytes 12296 | tf_op jit(solution)/shard_map/ppermute | solution.py:50
  48.5 16.5 %collective-permute-start.6 = (f32[1,1024]{1,0:T(1,128)S(1)}, f32[1,1024]{1,0:T(1,128)S(1)}, u32[]{:S(2)}, u32[]{:S(2)}) collective-permute-start(f32[1,1024]{1,0:T(1,128)S(1)} %get-tuple-element.874), channel_id=1, source_target_pairs={{4,0},{8,4},{12,8},{16,12},{20,16},{24,20},{28,24},{32,28},{36,32}... | collective-permute-start | bytes 12296 | tf_op jit(solution)/shard_map/ppermute | solution.py:50
  55.4 31.5 %collective-permute-start.9 = (bf16[2,1024,256]{2,1,0:T(8,128)(2,1)}, bf16[2,1024,256]{2,1,0:T(8,128)(2,1)}, u32[]{:S(2)}, u32[]{:S(2)}) collective-permute-start(bf16[2,1024,256]{2,1,0:T(8,128)(2,1)} %get-tuple-element.843), channel_id=1, source_target_pairs={{0,8},{4,12},{8,16},{12,20},{16,24},{20,28},{24,32},{28,36},{32,40... | collective-permute-start | bytes 3145736 | tf_op jit(solution)/shard_map/ppermute | solution.py:50
  57.5 23.2 %collective-permute-start.1 = (f32[2,1024]{1,0:T(2,128)S(1)}, f32[2,1024]{1,0:T(2,128)S(1)}, u32[]{:S(2)}, u32[]{:S(2)}) collective-permute-start(f32[2,1024]{1,0:T(2,128)S(1)} %get-tuple-element.879), channel_id=1, source_target_pairs={{0,8},{4,12},{8,16},{12,20},{16,24},{20,28},{24,32},{28,36},{32,40... | collective-permute-start | bytes 24584 | tf_op jit(solution)/shard_map/ppermute | solution.py:50
  59.5 21.3 %collective-permute-start.3 = (f32[2,1024]{1,0:T(2,128)S(1)}, f32[2,1024]{1,0:T(2,128)S(1)}, u32[]{:S(2)}, u32[]{:S(2)}) collective-permute-start(f32[2,1024]{1,0:T(2,128)S(1)} %get-tuple-element.878), channel_id=1, source_target_pairs={{8,0},{12,4},{16,8},{20,12},{24,16},{28,20},{32,24},{36,28},{40,32... | collective-permute-start | bytes 24584 | tf_op jit(solution)/shard_map/ppermute | solution.py:50
  81.1 27.7 %collective-permute-start.11 = (bf16[2,1024,256]{2,1,0:T(8,128)(2,1)S(1)}, bf16[2,1024,256]{2,1,0:T(8,128)(2,1)S(1)}, u32[]{:S(2)}, u32[]{:S(2)}) collective-permute-start(bf16[2,1024,256]{2,1,0:T(8,128)(2,1)S(1)} %get-tuple-element.842), channel_id=1, source_target_pairs={{8,0},{12,4},{16,8},{20,12},{24,16},{28,20},{32,24},{36,28},{40,32... | collective-permute-start | bytes 3145736 | tf_op jit(solution)/shard_map/ppermute | solution.py:50
  298.2 18.4 %collective-permute-start.12 = (f32[4,256]{1,0:T(4,128)S(1)}, f32[4,256]{1,0:T(4,128)S(1)}, u32[]{:S(2)}, u32[]{:S(2)}) collective-permute-start(f32[4,256]{1,0:T(4,128)S(1)} %get-tuple-element.860), channel_id=1, source_target_pairs={{12,0},{16,4},{20,8},{24,12},{28,16},{32,20},{36,24},{40,28},{44,3... | collective-permute-start | bytes 12296 | tf_op jit(solution)/shard_map/ppermute | solution.py:50
  307.6 16.7 %collective-permute-start.14 = (f32[4,256]{1,0:T(4,128)S(1)}, f32[4,256]{1,0:T(4,128)S(1)}, u32[]{:S(2)}, u32[]{:S(2)}) collective-permute-start(f32[4,256]{1,0:T(4,128)S(1)} %get-tuple-element.864), channel_id=1, source_target_pairs={{4,0},{8,4},{12,8},{16,12},{20,16},{24,20},{28,24},{32,28},{36,32}... | collective-permute-start | bytes 12296 | tf_op jit(solution)/shard_map/ppermute | solution.py:50
  310.0 16.3 %collective-permute-start.15 = (f32[4,256]{1,0:T(4,128)S(1)}, f32[4,256]{1,0:T(4,128)S(1)}, u32[]{:S(2)}, u32[]{:S(2)}) collective-permute-start(f32[4,256]{1,0:T(4,128)S(1)} %get-tuple-element.863), channel_id=1, source_target_pairs={{0,4},{4,8},{8,12},{12,16},{16,20},{20,24},{24,28},{28,32},{32,36}... | collective-permute-start | bytes 12296 | tf_op jit(solution)/shard_map/ppermute | solution.py:50
  313.2 15.6 %collective-permute-start.16 = (f32[4,256]{1,0:T(4,128)S(1)}, f32[4,256]{1,0:T(4,128)S(1)}, u32[]{:S(2)}, u32[]{:S(2)}) collective-permute-start(f32[4,256]{1,0:T(4,128)S(1)} %get-tuple-element.862), channel_id=1, source_target_pairs={{0,8},{4,12},{8,16},{12,20},{16,24},{20,28},{24,32},{28,36},{32,40... | collective-permute-start | bytes 12296 | tf_op jit(solution)/shard_map/ppermute | solution.py:50
  318.6 16.7 %collective-permute-start.18 = (f32[4,256]{1,0:T(4,128)S(1)}, f32[4,256]{1,0:T(4,128)S(1)}, u32[]{:S(2)}, u32[]{:S(2)}) collective-permute-start(f32[4,256]{1,0:T(4,128)S(1)} %get-tuple-element.866), channel_id=1, source_target_pairs={{12,0},{16,4},{20,8},{24,12},{28,16},{32,20},{36,24},{40,28},{44,3... | collective-permute-start | bytes 12296 | tf_op jit(solution)/shard_map/ppermute | solution.py:50
  350.0 16.3 %collective-permute-start.24 = (f32[1024]{0:T(1024)S(1)}, f32[1024]{0:T(1024)S(1)}, u32[]{:S(2)}, u32[]{:S(2)}) collective-permute-start(f32[1024]{0:T(1024)S(1)} %bitcast.212), channel_id=1, source_target_pairs={{0,12},{4,16},{8,20},{12,24},{16,28},{20,32},{24,36},{28,40},{32,4... | collective-permute-start | bytes 12296 | tf_op jit(solution)/shard_map/ppermute | solution.py:50
  352.1 17.7 %collective-permute-start.25 = (f32[1024]{0:T(1024)S(1)}, f32[1024]{0:T(1024)S(1)}, u32[]{:S(2)}, u32[]{:S(2)}) collective-permute-start(f32[1024]{0:T(1024)S(1)} %bitcast.213), channel_id=1, source_target_pairs={{0,8},{4,12},{8,16},{12,20},{16,24},{20,28},{24,32},{28,36},{32,40... | collective-permute-start | bytes 12296 | tf_op jit(solution)/shard_map/ppermute | solution.py:50
  354.0 15.8 %collective-permute-start.26 = (f32[1024]{0:T(1024)S(1)}, f32[1024]{0:T(1024)S(1)}, u32[]{:S(2)}, u32[]{:S(2)}) collective-permute-start(f32[1024]{0:T(1024)S(1)} %bitcast.214), channel_id=1, source_target_pairs={{0,4},{4,8},{8,12},{12,16},{16,20},{20,24},{24,28},{28,32},{32,36}... | collective-permute-start | bytes 12296 | tf_op jit(solution)/shard_map/ppermute | solution.py:50
  555.3 16.3 %collective-permute-start.30 = (f32[4,256]{1,0:T(4,128)S(1)}, f32[4,256]{1,0:T(4,128)S(1)}, u32[]{:S(2)}, u32[]{:S(2)}) collective-permute-start(f32[4,256]{1,0:T(4,128)S(1)} %get-tuple-element.846), channel_id=1, source_target_pairs={{12,0},{16,4},{20,8},{24,12},{28,16},{32,20},{36,24},{40,28},{44,3... | collective-permute-start | bytes 12296 | tf_op jit(solution)/shard_map/ppermute | solution.py:50
  562.7 16.7 %collective-permute-start.32 = (f32[4,256]{1,0:T(4,128)S(1)}, f32[4,256]{1,0:T(4,128)S(1)}, u32[]{:S(2)}, u32[]{:S(2)}) collective-permute-start(f32[4,256]{1,0:T(4,128)S(1)} %get-tuple-element.850), channel_id=1, source_target_pairs={{4,0},{8,4},{12,8},{16,12},{20,16},{24,20},{28,24},{32,28},{36,32}... | collective-permute-start | bytes 12296 | tf_op jit(solution)/shard_map/ppermute | solution.py:50
  564.7 16.8 %collective-permute-start.33 = (f32[4,256]{1,0:T(4,128)S(1)}, f32[4,256]{1,0:T(4,128)S(1)}, u32[]{:S(2)}, u32[]{:S(2)}) collective-permute-start(f32[4,256]{1,0:T(4,128)S(1)} %get-tuple-element.849), channel_id=1, source_target_pairs={{0,4},{4,8},{8,12},{12,16},{16,20},{20,24},{24,28},{28,32},{32,36}... | collective-permute-start | bytes 12296 | tf_op jit(solution)/shard_map/ppermute | solution.py:50
  568.3 15.3 %collective-permute-start.34 = (f32[4,256]{1,0:T(4,128)S(1)}, f32[4,256]{1,0:T(4,128)S(1)}, u32[]{:S(2)}, u32[]{:S(2)}) collective-permute-start(f32[4,256]{1,0:T(4,128)S(1)} %get-tuple-element.848), channel_id=1, source_target_pairs={{0,8},{4,12},{8,16},{12,20},{16,24},{20,28},{24,32},{28,36},{32,40... | collective-permute-start | bytes 12296 | tf_op jit(solution)/shard_map/ppermute | solution.py:50
  571.6 15.5 %collective-permute-start.35 = (f32[4,256]{1,0:T(4,128)S(1)}, f32[4,256]{1,0:T(4,128)S(1)}, u32[]{:S(2)}, u32[]{:S(2)}) collective-permute-start(f32[4,256]{1,0:T(4,128)S(1)} %get-tuple-element.847), channel_id=1, source_target_pairs={{0,12},{4,16},{8,20},{12,24},{16,28},{20,32},{24,36},{28,40},{32,4... | collective-permute-start | bytes 12296 | tf_op jit(solution)/shard_map/ppermute | solution.py:50
  573.8 16.7 %collective-permute-start.36 = (f32[4,256]{1,0:T(4,128)S(1)}, f32[4,256]{1,0:T(4,128)S(1)}, u32[]{:S(2)}, u32[]{:S(2)}) collective-permute-start(f32[4,256]{1,0:T(4,128)S(1)} %get-tuple-element.852), channel_id=1, source_target_pairs={{12,0},{16,4},{20,8},{24,12},{28,16},{32,20},{36,24},{40,28},{44,3... | collective-permute-start | bytes 12296 | tf_op jit(solution)/shard_map/ppermute | solution.py:50
  (23 other events, 276.3 us)
where the time goes:
time: 613 us; the launch traced here: 606 us
  loops' own time  191 us (31%)
  starting transfers between devices  149 us (24%)
  matrix products  108 us (18%)
  local copies, waits for them, and re-layouts  44.5 us (7%)
  other arithmetic  42.4 us (7%)
  waiting for transfers between devices  41.5 us (7%)
  blocking collectives  28.3 us (5%)
    ppermute x42, starting transfers between devices, shifted(): return lax.ppermute(block, axis, route)  146 us
    dot_general x96, matrix products, inner_tile(): lax.dot_general(lefts[member], rights[member], (((1,), (1,)), ((), ())),...  108 us
    another operation x2, loops' own time, on_device(): lax.scan(column_step, initial, (pair_spots, pair_rows, pair_active, stored))  95.8 us
    another operation x2, loops' own time, on_device(): lax.scan(row_step, row_initial, (pair_spots, pair_rows, pair_active))  95 us
    ppermute x42, waiting for transfers between devices, shifted(): return lax.ppermute(block, axis, route)  37.2 us
    slice x48, local copies, waits for them, and re-layouts, pick_two(): index_pair[member]  27.1 us
    all_to_all x2, blocking collectives, from_everyone(): lax.all_to_all(jnp.broadcast_to(array[None], (peers, *array.shape)), axis...  20.1 us
  transfers between devices with their start and end apart: 43, of which 9 were waited for; matrix products, arithmetic and copies ran while one was open for 2% of the time, Pallas kernels for 0%

commit v1 on v0

v1 whole, which is shorter than its diff:
```python
import functools
import math

import jax
import jax.numpy as jnp
from jax import lax
from jax.experimental import pallas as pl
from jax.experimental.pallas import tpu as pltpu
from jax.sharding import PartitionSpec as P

REACH = 3
WIDE = 2 * REACH
SPOTS = 2 * REACH + 1
BLOCK = 256
LOG2E = 1.0 / math.log(2.0)
SCALE = 4.0 * LOG2E
NEG = -1e30
MESH = pl.DeviceIdType.MESH
F32 = jnp.float32


def tree(op, values):
    values = list(values)
    while len(values) > 1:
        paired = [op(a, b) for a, b in zip(values[::2], values[1::2])]
        values = paired + values[len(paired) * 2 :]
    return values[0]


def log2(x):
    return jnp.log(x) * LOG2E


def half_norms(points):
    wide = points.astype(F32)
    square = wide * wide
    high = square.astype(jnp.bfloat16)
    low = (square - high.astype(F32)).astype(jnp.bfloat16)
    ones = jnp.ones((8, points.shape[1]), jnp.bfloat16)
    dims = (((1,), (1,)), ((), ()))
    total = lax.dot_general(ones, high, dims, preferred_element_type=F32)
    total += lax.dot_general(ones, low, dims, preferred_element_type=F32)
    return 0.5 * total


def kernel(
    n_pts,
    n_help,
    src_hbm,
    dst_hbm,
    src_lw,
    dst_lw,
    init_g,
    lists,
    counts,
    out_f,
    out_g,
    xs,
    ys,
    vin,
    yout,
    yin,
    dots,
    peak,
    total,
    bvec,
    acol,
    lsend,
    lrecv,
    gsend,
    grecv,
    glast,
    local_sem,
    xs_send,
    xs_recv,
    ys_send,
    ys_recv,
    vec_send,
    vec_recv,
    row_send,
    row_recv,
    f_send,
    f_recv,
    g_send,
    g_recv,
    e_send,
    e_recv,
):
    p = lax.axis_index("pts")
    h = lax.axis_index("help")
    near = [d for d in range(-REACH, REACH + 1) if d]
    wide = [d for d in range(-WIDE, WIDE + 1) if d]

    def there(d):
        return (p + d >= 0) & (p + d < n_pts)

    def when_there(d, do):
        @pl.when(there(d))
        def _():
            do()

    def helper(j):
        return lax.rem(h + j, n_help)

    def remote(src, dst, send, recv, device):
        return pltpu.make_async_remote_copy(
            src_ref=src,
            dst_ref=dst,
            send_sem=send,
            recv_sem=recv,
            device_id=device,
            device_id_type=MESH,
        )

    for d in near:

        @pl.when(jnp.logical_not(there(d)))
        def _():
            ys[d + REACH] = jnp.zeros(ys.shape[1:], ys.dtype)
            vin[d + REACH] = jnp.zeros(vin.shape[1:], F32)
            glast[d + REACH] = jnp.full(glast.shape[1:], NEG, F32)

    for d in wide:

        @pl.when(jnp.logical_not(there(d)))
        def _():
            for k in range(SPOTS):
                grecv[k, d + WIDE] = jnp.full(grecv.shape[2:], NEG, F32)

    barrier = pltpu.get_barrier_semaphore()
    for j in range(1, n_help):
        pl.semaphore_signal(barrier, inc=1, device_id={"help": helper(j)}, device_id_type=MESH)
    for d in wide:
        when_there(
            d,
            lambda d=d: pl.semaphore_signal(
                barrier, inc=1, device_id={"pts": p + d}, device_id_type=MESH
            ),
        )

    get_dst = pltpu.make_async_copy(dst_hbm, ys.at[REACH], local_sem.at[0])
    get_src = pltpu.make_async_copy(src_hbm, xs.at[h], local_sem.at[1])
    get_dst.start()
    get_src.start()

    lane = lax.broadcasted_iota(jnp.int32, (8, 128), 1)
    sub = lax.broadcasted_iota(jnp.int32, (8, 128), 0)
    listed = lists[...]
    width = listed.shape[1]
    slot = lax.broadcasted_iota(jnp.int32, (8, width), 1)
    spot = lax.broadcasted_iota(jnp.int32, (8, width), 0)
    live = slot < counts[0]
    for c in range(n_help):
        column = (p + spot - REACH) * n_help + c
        hit = jnp.where((listed == column) & live, 1.0, 0.0)
        yout[c, 0:8, :] = jnp.broadcast_to(jnp.max(hit, axis=1, keepdims=True), (8, 128))
        yout[c, 8:16, :] = jnp.broadcast_to(
            jnp.concatenate([src_lw[...] * LOG2E] * 4, axis=0), (8, 128)
        )

    get_dst.wait()
    dst_half = half_norms(ys[REACH])
    vin[REACH, 0:1, :] = dst_lw[0:1, :] * LOG2E + SCALE * (init_g[0:1, :] - dst_half[0:1, 0:128])
    vin[REACH, 1:2, :] = dst_lw[1:2, :] * LOG2E + SCALE * (init_g[1:2, :] - dst_half[0:1, 128:256])
    vin[REACH, 2:4, :] = dst_lw[...] * LOG2E
    get_src.wait()
    src_half = half_norms(xs[h])

    pl.semaphore_wait(
        barrier,
        n_help - 1 + jnp.minimum(p, WIDE) + jnp.minimum(n_pts - 1 - p, WIDE),
    )

    def vec_copy(d):
        return remote(
            vin.at[REACH], vin.at[REACH - d], vec_send.at[d + REACH], vec_recv.at[REACH - d], {"pts": p + d}
        )

    def ys_copy(d):
        return remote(
            ys.at[REACH], ys.at[REACH - d], ys_send.at[d + REACH], ys_recv.at[REACH - d], {"pts": p + d}
        )

    def row_copy(j):
        return remote(
            yout.at[helper(j)], yin.at[h], row_send.at[j], row_recv.at[j], {"help": helper(j)}
        )

    def xs_copy(j):
        return remote(xs.at[h], xs.at[h], xs_send.at[j], xs_recv.at[j], {"help": helper(j)})

    steps = [1, -1, 2, -2, 3, -3]
    for j in range(1, n_help):
        row_copy(j).start()
    for d in steps:
        when_there(d, lambda d=d: vec_copy(d).start())
    for j in range(1, n_help):
        xs_copy(j).start()
    for d in steps:
        when_there(d, lambda d=d: ys_copy(d).start())
    yin[h] = yout[h]

    for j in range(1, n_help):
        xs_copy(j).wait_recv()

    def one_spot(step, carry):
        odd = lax.rem(step, 2)
        away = (step + 1) // 2 * (1 - 2 * odd)
        k = REACH + away

        @pl.when((step > 0) & (p + away >= 0) & (p + away < n_pts))
        def _():
            remote(ys.at[REACH], ys.at[k], ys_send.at[k], ys_recv.at[k], {"pts": p + away}).wait_recv()

        for r in range(n_help):
            inner = lax.dot_general(
                xs[r], ys[k], (((1,), (1,)), ((), ())), preferred_element_type=F32
            )
            inner = inner * SCALE
            dots[k, 2 * r] = inner[0:128]
            dots[k, 2 * r + 1] = inner[128:256]
        return carry

    lax.fori_loop(0, SPOTS, one_spot, 0)

    for j in range(1, n_help):
        row_copy(j).wait_recv()
    for d in steps:
        when_there(d, lambda d=d: vec_copy(-d).wait_recv())
    for k in range(SPOTS):
        bvec[k] = vin[k, 0:2, :]

    diagonal = lane - sub

    def row_sweep():
        def one(rh, carry):
            r = rh // 2
            push = []
            for k in range(SPOTS):
                on = yin[r, k : k + 1, :] > 0.5
                for j in range(2):
                    row = jnp.where(on, bvec[k, j : j + 1, :], NEG)
                    push.append(jnp.broadcast_to(row, (8, 128)))
            found = jnp.zeros((8, 128), F32)
            for g in range(16):
                t = [
                    dots[k, rh, 8 * g : 8 * g + 8, 128 * j : 128 * j + 128] + push[2 * k + j]
                    for k in range(SPOTS)
                    for j in range(2)
                ]
                top = tree(jnp.maximum, t)
                s = tree(jnp.add, [jnp.exp2(v - top) for v in t])
                most = jnp.max(top, axis=1, keepdims=True)
                whole = jnp.sum(s * jnp.exp2(top - most), axis=1, keepdims=True)
                found = jnp.where(diagonal == 8 * g, most + log2(whole), found)
            lsend[pl.ds(rh, 1), :] = jnp.sum(found, axis=0, keepdims=True)
            return carry

        lax.fori_loop(0, 2 * n_help, one, 0)

    def column_sweep():
        def one(rh, carry):
            row = jnp.broadcast_to(acol[pl.ds(rh, 1), :], (8, 128))
            lift = [
                jnp.broadcast_to(
                    jnp.sum(jnp.where(diagonal == 8 * g, row, 0.0), axis=1, keepdims=True),
                    (8, 128),
                )
                for g in range(16)
            ]
            for k in range(SPOTS):
                for j in range(2):
                    u = [
                        dots[k, rh, 8 * g : 8 * g + 8, 128 * j : 128 * j + 128] + lift[g]
                        for g in range(16)
                    ]
                    top = tree(jnp.maximum, u)
                    peak[2 * k + j, rh] = top
                    total[2 * k + j, rh] = tree(jnp.add, [jnp.exp2(v - top) for v in u])
            return carry

        lax.fori_loop(0, 2 * n_help, one, 0)

        def close(k, carry):
            for j in range(2):
                tops = [
                    jnp.where(yin[rh // 2, pl.ds(k, 1), :] > 0.5, peak[2 * k + j, rh], NEG)
                    for rh in range(2 * n_help)
                ]
                top = tree(jnp.maximum, tops)
                most = jnp.max(top, axis=0, keepdims=True)
                s = tree(
                    jnp.add,
                    [total[2 * k + j, rh] * jnp.exp2(tops[rh] - most) for rh in range(2 * n_help)],
                )
                gsend[k, j : j + 1, :] = most + log2(jnp.sum(s, axis=0, keepdims=True))
            return carry

        lax.fori_loop(0, SPOTS, close, 0)

    def fold(parts):
        top = tree(jnp.maximum, parts)
        return top + log2(tree(jnp.add, [jnp.exp2(v - top) for v in parts]))

    def f_copy(it, j):
        return remote(
            lsend.at[it], lrecv.at[it, j], f_send.at[it, j], f_recv.at[it, j], {"help": helper(j)}
        )

    def g_copy(d):
        low, count = max(0, d), SPOTS - abs(d)
        return remote(
            gsend.at[0, pl.ds(low, count)],
            grecv.at[pl.ds(low, count), WIDE - d],
            g_send.at[d + WIDE],
            g_recv.at[WIDE - d],
            {"pts": p + d},
        )

    def e_copy(d):
        return remote(
            gsend.at[1, d + REACH],
            glast.at[REACH - d],
            e_send.at[d + REACH],
            e_recv.at[REACH - d],
            {"pts": p + d},
        )

    lsend_all, gsend_all = lsend, gsend
    for it in range(2):
        lsend, gsend = lsend_all.at[it], gsend_all.at[it]
        row_sweep()
        lsend, gsend = lsend_all, gsend_all
        for j in range(1, n_help):
            f_copy(it, j).start()
        for j in range(1, n_help):
            f_copy(it, j).wait_recv()
        force = -fold([lsend[it]] + [lrecv[it, j] for j in range(1, n_help)])
        for r in range(n_help):
            acol[2 * r : 2 * r + 2, :] = force[2 * r : 2 * r + 2, :] + yin[r, 8:10, :]
        if it == 1:
            lrecv[1, 0] = force
            out_f[0:1, :] = lrecv[1, 0, pl.ds(2 * h, 1), :] * (1.0 / SCALE) + src_half[0:1, 0:128]
            out_f[1:2, :] = (
                lrecv[1, 0, pl.ds(2 * h + 1, 1), :] * (1.0 / SCALE) + src_half[0:1, 128:256]
            )
        lsend, gsend = lsend_all.at[it], gsend_all.at[it]
        column_sweep()
        lsend, gsend = lsend_all, gsend_all
        if it == 0:
            for d in wide:
                when_there(d, lambda d=d: g_copy(d).start())
            for k in range(SPOTS):
                grecv[k, WIDE] = gsend[0, k]
            for d in wide:
                when_there(d, lambda d=d: g_copy(-d).wait_recv())
            for k in range(SPOTS):
                parts = [grecv[REACH - e, k + REACH + e] for e in range(-REACH, REACH + 1)]
                bvec[k] = vin[k, 2:4, :] - fold(parts)
        else:
            for d in near:
                when_there(d, lambda d=d: e_copy(d).start())
            glast[REACH] = gsend[1, REACH]
            for d in near:
                when_there(d, lambda d=d: e_copy(-d).wait_recv())
            pot = -fold([glast[k] for k in range(SPOTS)]) * (1.0 / SCALE)
            out_g[0:1, :] = pot[0:1, :] + dst_half[0:1, 0:128]
            out_g[1:2, :] = pot[1:2, :] + dst_half[0:1, 128:256]

    for j in range(1, n_help):
        row_copy(j).wait_send()
        xs_copy(j).wait_send()
        for it in range(2):
            f_copy(it, j).wait_send()
    for d in near:

        @pl.when(there(d))
        def _(d=d):
            vec_copy(d).wait_send()
            ys_copy(d).wait_send()
            e_copy(d).wait_send()

    for d in wide:
        when_there(d, lambda d=d: g_copy(d).wait_send())


def solution(mesh):
    n_pts, n_help = mesh.shape["pts"], mesh.shape["help"]

    def on_device(src_points, dst_points, src_logw, dst_logw, init_g, pair_lists, pair_counts):
        dim = src_points.shape[1]
        vmem = pl.BlockSpec(memory_space=pltpu.VMEM)
        dma = pltpu.SemaphoreType.DMA
        bf16 = jnp.bfloat16
        out = jax.ShapeDtypeStruct((2, 128), F32)
        f, g = pl.pallas_call(
            functools.partial(kernel, n_pts, n_help),
            out_shape=(out, out),
            in_specs=[
                pl.BlockSpec(memory_space=pl.ANY),
                pl.BlockSpec(memory_space=pl.ANY),
                vmem,
                vmem,
                vmem,
                vmem,
                pl.BlockSpec(memory_space=pltpu.SMEM),
            ],
            out_specs=(vmem, vmem),
            scratch_shapes=[
                pltpu.VMEM((n_help, BLOCK, dim), bf16),
                pltpu.VMEM((SPOTS, BLOCK, dim), bf16),
                pltpu.VMEM((SPOTS, 4, 128), F32),
                pltpu.VMEM((n_help, 16, 128), F32),
                pltpu.VMEM((n_help, 16, 128), F32),
                pltpu.VMEM((SPOTS, 2 * n_help, 128, BLOCK), F32),
                pltpu.VMEM((2 * SPOTS, 2 * n_help, 8, 128), F32),
                pltpu.VMEM((2 * SPOTS, 2 * n_help, 8, 128), F32),
                pltpu.VMEM((SPOTS, 2, 128), F32),
                pltpu.VMEM((2 * n_help, 128), F32),
                pltpu.VMEM((2, 2 * n_help, 128), F32),
                pltpu.VMEM((2, n_help, 2 * n_help, 128), F32),
                pltpu.VMEM((2, SPOTS, 2, 128), F32),
                pltpu.VMEM((SPOTS, 2 * WIDE + 1, 2, 128), F32),
                pltpu.VMEM((SPOTS, 2, 128), F32),
                dma((2,)),
                dma((n_help,)),
                dma((n_help,)),
                dma((SPOTS,)),
                dma((SPOTS,)),
                dma((SPOTS,)),
                dma((SPOTS,)),
                dma((n_help,)),
                dma((n_help,)),
                dma((2, n_help)),
                dma((2, n_help)),
                dma((2 * WIDE + 1,)),
                dma((2 * WIDE + 1,)),
                dma((SPOTS,)),
                dma((SPOTS,)),
            ],
            compiler_params=pltpu.CompilerParams(collective_id=0, has_side_effects=True),
            name="sinkhorn",
        )(
            src_points,
            dst_points,
            src_logw.reshape(2, 128),
            dst_logw.reshape(2, 128),
            init_g.reshape(2, 128),
            pair_lists,
            pair_counts,
        )
        return f.reshape(-1), g.reshape(-1)

    rows = P(("pts", "help"))
    blocks = P(("pts", "help"), None)
    return jax.shard_map(
        on_device,
        mesh=mesh,
        in_specs=(blocks, blocks, rows, rows, rows, blocks, rows),
        out_specs=(rows, rows),
        check_vma=False,
    )
```

time: 613 us -> 54.5 us (0.09); the launches traced: 606 us -> 54.1 us
  loops' own time: 191 us -> 0 us
  starting transfers between devices: 149 us -> 0 us
  matrix products: 108 us -> 0 us
  Pallas kernels: 0 us -> 51 us
  local copies, waits for them, and re-layouts: 44.5 us -> 1.86 us
  other arithmetic: 42.4 us -> 0 us
  waiting for transfers between devices: 41.5 us -> 0 us
  blocking collectives: 28.3 us -> 0 us
    another operation x4 -> x0, loops' own time: 191 us -> none  [the longest x2 95.8 us: on_device(): lax.scan(column_step, initial, (pair_spots, pair_rows, pair_active, stored))]
    ppermute x42 -> x0, starting transfers between devices: 146 us -> none  [shifted(): return lax.ppermute(block, axis, route)]
    dot_general x96 -> x0, matrix products: 108 us -> none  [inner_tile(): lax.dot_general(lefts[member], rights[member], (((1,), (1,)), ((), ())),...]
    pallas_call x0 -> x1, Pallas kernels: none -> 51 us  [on_device(): pl.pallas_call(functools.partial(kernel, n_pts, n_help), out_shape=(out,...]
    ppermute x42 -> x0, waiting for transfers between devices: 37.2 us -> none  [shifted(): return lax.ppermute(block, axis, route)]
    slice x57 -> x0, local copies, waits for them, and re-layouts: 27.3 us -> none  [the longest x48 27.1 us: pick_two(): index_pair[member]]
    all_to_all x2 -> x0, blocking collectives: 20.1 us -> none  [from_everyone(): lax.all_to_all(jnp.broadcast_to(array[None], (peers, *array.shape)), axis...]
    reduce_sum x50 -> x0, other arithmetic: 16.2 us -> none  [the longest x24 7.07 us: row_step(): tile_sum = jnp.sum(jnp.exp(scores - tile_top[:, :, None]), axis=2)]
  transfers between devices with their start and end apart: 43 -> 0, of which waited for: 9 -> 0; matrix products, arithmetic and copies ran while one was open for 2% -> 0% of each run, Pallas kernels for 0% -> 0%
where the time goes in v1:
time: 54.5 us; the launch traced here: 54.1 us
  Pallas kernels  51 us (94%)
  local copies, waits for them, and re-layouts  1.86 us (3%)
  between operations  1.3 us (2%)
    pallas_call x1, Pallas kernels, on_device(): pl.pallas_call(functools.partial(kernel, n_pts, n_help), out_shape=(out,...  51 us
    unnamed x6, local copies, waits for them, and re-layouts  1.86 us

profile of v1, /device:TPU:7, one launch (start us, length us, event | category | flops | bytes accessed | tf_op | source)
XLA Modules:
  0.0 54.1 jit_solution(10476097496228596467)
XLA Ops:
  1.3 51.0 %sinkhorn.1 = (f32[2,128]{1,0:T(2,128)}, f32[2,128]{1,0:T(2,128)}) custom-call(bf16[256,256]{1,0:T(8,128)(2,1)} %src_hbm.1, bf16[256,256]{1,0:T(8,128)(2,1)} %dst_hbm.1, f32[2,128]{1,0:T(2,128)} %bitcast.5, f32[2,128]{1,0:T(2,128)} %bitcast.6, f32[2,128]{1,0:T(2,128)} %bitcast.7, s32[1,24]{1,0:T(1,128)} %lists.1, s32[1]{0:T(128)S(6)} %copy.11.counts), custom_call_target="tpu_custom_call" | custom-call | tf_op jit(solution)/shard_map/sinkhorn/pallas_call | solution.py:396
  52.3 0.0 copy-start.1
  52.3 0.7 %copy-done.1 = f32[2,128]{1,0:T(2,128)S(1)} copy-done((f32[2,128]{1,0:T(2,128)S(1)}, f32[2,128]{1,0:T(2,128)}, u32[]{:S(2)}) %copy-start.1) | copy-done | bytes 1048
  52.9 0.0 copy-start
  52.9 0.6 %copy.12 = f32[256]{0:T(256)} copy(f32[256]{0:T(256)S(1)} %bitcast.9) | data formatting | bytes 2048
  53.5 0.1 copy-done
  53.6 0.6 %copy.13 = f32[256]{0:T(256)} copy(f32[256]{0:T(256)S(1)} %bitcast.8) | data formatting | bytes 2048
Async XLA Ops:
  52.3 0.7 %copy-start.1 = (f32[2,128]{1,0:T(2,128)S(1)}, f32[2,128]{1,0:T(2,128)}, u32[]{:S(2)}) copy-start(f32[2,128]{1,0:T(2,128)} %get-tuple-element.4) | copy-start | bytes 3076
  52.9 0.6 %copy-start = (f32[2,128]{1,0:T(2,128)S(1)}, f32[2,128]{1,0:T(2,128)}, u32[]{:S(2)}) copy-start(f32[2,128]{1,0:T(2,128)} %get-tuple-element.5) | copy-start | bytes 3076

commit v2 on v1

--- a/solution.py
+++ b/solution.py
@@ -71,10 +71,13 @@
     grecv,
     glast,
     local_sem,
-    xs_send,
-    xs_recv,
-    ys_send,
-    ys_recv,
+    x_send,
+    x_recv,
+    x_pass,
+    y_send,
+    y_recv,
+    y_pass,
+    y_far,
     vec_send,
     vec_recv,
     row_send,
@@ -112,6 +115,106 @@
             device_id_type=MESH,
         )
 
+    side = 1 - 2 * lax.rem(p, 2)
+
+    barrier = pltpu.get_barrier_semaphore()
+    for j in range(1, n_help):
+        pl.semaphore_signal(barrier, inc=1, device_id={"help": helper(j)}, device_id_type=MESH)
+    for d in near:
+        when_there(
+            d,
+            lambda d=d: pl.semaphore_signal(
+                barrier, inc=1, device_id={"pts": p + d}, device_id_type=MESH
+            ),
+        )
+
+    get_dst = pltpu.make_async_copy(dst_hbm, ys.at[REACH], local_sem.at[0])
+    get_src = pltpu.make_async_copy(src_hbm, xs.at[h], local_sem.at[1])
+    get_dst.start()
+    get_src.start()
+
+    with jax.named_scope("barrier"):
+        pl.semaphore_wait(
+            barrier,
+            n_help - 1 + jnp.minimum(p, REACH) + jnp.minimum(n_pts - 1 - p, REACH),
+        )
+
+    half = BLOCK // 2
+    parts = [pl.ds(0, half), pl.ds(half, half)]
+
+    ahead, behind = {"help": helper(1)}, {"help": helper(n_help - 1)}
+
+    def x_own(way, q):
+        return remote(
+            src_hbm.at[parts[q]],
+            xs.at[h, parts[q]],
+            x_send.at[way, q],
+            x_recv.at[way, q],
+            (ahead, behind)[way],
+        )
+
+    def x_on(way):
+        r = helper(n_help - 1 if way == 0 else 1)
+        here = xs.at[r, parts[way]]
+        return remote(here, here, x_pass.at[way], x_recv.at[2, way], (ahead, behind)[way])
+
+    def y_own(way, q):
+        d = (2, -2)[way]
+        return remote(
+            dst_hbm.at[parts[q]],
+            ys.at[REACH - d, parts[q]],
+            y_send.at[way, q],
+            y_recv.at[REACH - d, q],
+            {"pts": p + d},
+        )
+
+    def y_side():
+        return remote(
+            dst_hbm, ys.at[REACH - side], y_send.at[2, 0], y_recv.at[REACH - side, 0], {"pts": p + side}
+        )
+
+    def y_on(way, q):
+        d = (-2, 2)[way]
+        k = REACH + d - side
+        return remote(
+            ys.at[REACH + d, parts[q]],
+            ys.at[k, parts[q]],
+            y_pass.at[way, q],
+            y_recv.at[k, q],
+            {"pts": p + side},
+        )
+
+    def y_over(q):
+        k = REACH + 3 * side
+        return remote(
+            ys.at[REACH + 2 * side, parts[q]],
+            ys.at[k, parts[q]],
+            y_far.at[q],
+            y_recv.at[k, q],
+            {"pts": p - side},
+        )
+
+    def y_came(k, q):
+        return remote(
+            dst_hbm.at[parts[q]], ys.at[k, parts[q]], y_far.at[0], y_recv.at[k, q], {"pts": p + side}
+        )
+
+    def x_came(way, q):
+        r = helper((n_help - 1, 1, 2)[way])
+        return remote(
+            src_hbm.at[parts[q]], xs.at[r, parts[q]], x_pass.at[0], x_recv.at[way, q], ahead
+        )
+
+    x_own(0, 0).start()
+    x_own(1, 1).start()
+    when_there(2, lambda: y_own(0, 0).start())
+    when_there(-2, lambda: y_own(1, 0).start())
+    x_own(0, 1).start()
+    x_own(1, 0).start()
+    when_there(2, lambda: y_own(0, 1).start())
+    when_there(-2, lambda: y_own(1, 1).start())
+    y_side().start()
+
     for d in near:
 
         @pl.when(jnp.logical_not(there(d)))
@@ -126,22 +229,6 @@
         def _():
             for k in range(SPOTS):
                 grecv[k, d + WIDE] = jnp.full(grecv.shape[2:], NEG, F32)
-
-    barrier = pltpu.get_barrier_semaphore()
-    for j in range(1, n_help):
-        pl.semaphore_signal(barrier, inc=1, device_id={"help": helper(j)}, device_id_type=MESH)
-    for d in wide:
-        when_there(
-            d,
-            lambda d=d: pl.semaphore_signal(
-                barrier, inc=1, device_id={"pts": p + d}, device_id_type=MESH
-            ),
-        )
-
-    get_dst = pltpu.make_async_copy(dst_hbm, ys.at[REACH], local_sem.at[0])
-    get_src = pltpu.make_async_copy(src_hbm, xs.at[h], local_sem.at[1])
-    get_dst.start()
-    get_src.start()
 
     lane = lax.broadcasted_iota(jnp.int32, (8, 128), 1)
     sub = lax.broadcasted_iota(jnp.int32, (8, 128), 0)
@@ -163,70 +250,95 @@
     vin[REACH, 0:1, :] = dst_lw[0:1, :] * LOG2E + SCALE * (init_g[0:1, :] - dst_half[0:1, 0:128])
     vin[REACH, 1:2, :] = dst_lw[1:2, :] * LOG2E + SCALE * (init_g[1:2, :] - dst_half[0:1, 128:256])
     vin[REACH, 2:4, :] = dst_lw[...] * LOG2E
-    get_src.wait()
-    src_half = half_norms(xs[h])
-
-    pl.semaphore_wait(
-        barrier,
-        n_help - 1 + jnp.minimum(p, WIDE) + jnp.minimum(n_pts - 1 - p, WIDE),
-    )
 
     def vec_copy(d):
         return remote(
             vin.at[REACH], vin.at[REACH - d], vec_send.at[d + REACH], vec_recv.at[REACH - d], {"pts": p + d}
         )
 
-    def ys_copy(d):
-        return remote(
-            ys.at[REACH], ys.at[REACH - d], ys_send.at[d + REACH], ys_recv.at[REACH - d], {"pts": p + d}
-        )
-
     def row_copy(j):
         return remote(
             yout.at[helper(j)], yin.at[h], row_send.at[j], row_recv.at[j], {"help": helper(j)}
         )
-
-    def xs_copy(j):
-        return remote(xs.at[h], xs.at[h], xs_send.at[j], xs_recv.at[j], {"help": helper(j)})
 
     steps = [1, -1, 2, -2, 3, -3]
     for j in range(1, n_help):
         row_copy(j).start()
     for d in steps:
         when_there(d, lambda d=d: vec_copy(d).start())
-    for j in range(1, n_help):
-        xs_copy(j).start()
-    for d in steps:
-        when_there(d, lambda d=d: ys_copy(d).start())
     yin[h] = yout[h]
-
-    for j in range(1, n_help):
-        xs_copy(j).wait_recv()
-
-    def one_spot(step, carry):
-        odd = lax.rem(step, 2)
-        away = (step + 1) // 2 * (1 - 2 * odd)
-        k = REACH + away
-
-        @pl.when((step > 0) & (p + away >= 0) & (p + away < n_pts))
-        def _():
-            remote(ys.at[REACH], ys.at[k], ys_send.at[k], ys_recv.at[k], {"pts": p + away}).wait_recv()
-
-        for r in range(n_help):
+    get_src.wait()
+    src_half = half_norms(xs[h])
+
+    with jax.named_scope("relay"):
+        x_came(0, 0).wait_recv()
+        x_on(0).start()
+        x_came(1, 1).wait_recv()
+        x_on(1).start()
+        for q in range(2):
+            for way, d in enumerate((-2, 2)):
+
+                @pl.when(there(d))
+                def _(way=way, d=d, q=q):
+                    y_came(REACH + d, q).wait_recv()
+
+                    @pl.when((2 * side == d) & there(-side))
+                    def _():
+                        y_over(q).start()
+
+                    y_on(way, q).start()
+
+        x_came(0, 1).wait_recv()
+        x_came(1, 0).wait_recv()
+        remote(dst_hbm, ys.at[REACH + side], y_far.at[0], y_recv.at[REACH + side, 0], {"pts": p + side}).wait_recv()
+
+    def tiles(k, rows):
+        for r in rows:
             inner = lax.dot_general(
                 xs[r], ys[k], (((1,), (1,)), ((), ())), preferred_element_type=F32
             )
             inner = inner * SCALE
-            dots[k, 2 * r] = inner[0:128]
-            dots[k, 2 * r + 1] = inner[128:256]
+            dots[k, 2 * r] = inner[0:half]
+            dots[k, 2 * r + 1] = inner[half:]
+
+    def first(c):
+        return lax.select(c < 2, REACH + c * side, REACH + 10 - 4 * c)
+
+    def one_first(c, carry):
+        tiles(first(c), [helper(j) for j in (0, 1, 3)])
         return carry
 
-    lax.fori_loop(0, SPOTS, one_spot, 0)
-
-    for j in range(1, n_help):
-        row_copy(j).wait_recv()
-    for d in steps:
-        when_there(d, lambda d=d: vec_copy(-d).wait_recv())
+    def one_second(c, carry):
+        tiles(first(c), [helper(2)])
+        return carry
+
+    def one_third(c, carry):
+        d = lax.select(c < 2, side - 2 + 4 * c, -3 * side)
+        k = REACH + d
+
+        @pl.when(there(d))
+        def _():
+            for q in range(2):
+                y_came(k, q).wait_recv()
+
+        tiles(k, range(n_help))
+        return carry
+
+    with jax.named_scope("tiles1"):
+        lax.fori_loop(0, 4, one_first, 0)
+    with jax.named_scope("xlast"):
+        x_came(2, 0).wait_recv()
+        x_came(2, 1).wait_recv()
+    with jax.named_scope("tiles2"):
+        lax.fori_loop(0, 4, one_second, 0)
+    with jax.named_scope("tiles3"):
+        lax.fori_loop(0, 3, one_third, 0)
+
+    with jax.named_scope("vec"):
+        for j in range(1, n_help):
+            row_copy(j).wait_recv()
+        for d in steps:
+            when_there(d, lambda d=d: vec_copy(-d).wait_recv())
     for k in range(SPOTS):
         bvec[k] = vin[k, 0:2, :]
 
@@ -329,12 +441,14 @@
     lsend_all, gsend_all = lsend, gsend
     for it in range(2):
         lsend, gsend = lsend_all.at[it], gsend_all.at[it]
-        row_sweep()
+        with jax.named_scope('rows'):
+            row_sweep()
         lsend, gsend = lsend_all, gsend_all
         for j in range(1, n_help):
             f_copy(it, j).start()
-        for j in range(1, n_help):
-            f_copy(it, j).wait_recv()
+        with jax.named_scope('fwait'):
+            for j in range(1, n_help):
+                f_copy(it, j).wait_recv()
         force = -fold([lsend[it]] + [lrecv[it, j] for j in range(1, n_help)])
         for r in range(n_help):
             acol[2 * r : 2 * r + 2, :] = force[2 * r : 2 * r + 2, :] + yin[r, 8:10, :]
@@ -345,39 +459,50 @@
                 lrecv[1, 0, pl.ds(2 * h + 1, 1), :] * (1.0 / SCALE) + src_half[0:1, 128:256]
             )
         lsend, gsend = lsend_all.at[it], gsend_all.at[it]
-        column_sweep()
+        with jax.named_scope('cols'):
+            column_sweep()
         lsend, gsend = lsend_all, gsend_all
         if it == 0:
             for d in wide:
                 when_there(d, lambda d=d: g_copy(d).start())
             for k in range(SPOTS):
                 grecv[k, WIDE] = gsend[0, k]
-            for d in wide:
-                when_there(d, lambda d=d: g_copy(-d).wait_recv())
+            with jax.named_scope('gwait'):
+                for d in wide:
+                    when_there(d, lambda d=d: g_copy(-d).wait_recv())
             for k in range(SPOTS):
-                parts = [grecv[REACH - e, k + REACH + e] for e in range(-REACH, REACH + 1)]
-                bvec[k] = vin[k, 2:4, :] - fold(parts)
+                came = [grecv[REACH - e, k + REACH + e] for e in range(-REACH, REACH + 1)]
+                bvec[k] = vin[k, 2:4, :] - fold(came)
         else:
             for d in near:
                 when_there(d, lambda d=d: e_copy(d).start())
             glast[REACH] = gsend[1, REACH]
-            for d in near:
-                when_there(d, lambda d=d: e_copy(-d).wait_recv())
+            with jax.named_scope('ewait'):
+                for d in near:
+                    when_there(d, lambda d=d: e_copy(-d).wait_recv())
             pot = -fold([glast[k] for k in range(SPOTS)]) * (1.0 / SCALE)
             out_g[0:1, :] = pot[0:1, :] + dst_half[0:1, 0:128]
             out_g[1:2, :] = pot[1:2, :] + dst_half[0:1, 128:256]
 
     for j in range(1, n_help):
         row_copy(j).wait_send()
-        xs_copy(j).wait_send()
         for it in range(2):
             f_copy(it, j).wait_send()
+    for way in range(2):
+        x_on(way).wait_send()
+        for q in range(2):
+            x_own(way, q).wait_send()
+    y_side().wait_send()
+    for q in range(2):
+        for way, d in enumerate((2, -2)):
+            when_there(d, lambda way=way, q=q: y_own(way, q).wait_send())
+            when_there(-d, lambda way=way, q=q: y_on(way, q).wait_send())
+        pl.when(there(2 * side) & there(-side))(lambda q=q: y_over(q).wait_send())
     for d in near:
 
         @pl.when(there(d))
         def _(d=d):
             vec_copy(d).wait_send()
-            ys_copy(d).wait_send()
             e_copy(d).wait_send()
 
     for d in wide:
@@ -423,10 +548,13 @@
                 pltpu.VMEM((SPOTS, 2 * WIDE + 1, 2, 128), F32),
                 pltpu.VMEM((SPOTS, 2, 128), F32),
                 dma((2,)),
-                dma((n_help,)),
-                dma((n_help,)),
-                dma((SPOTS,)),
-                dma((SPOTS,)),
+                dma((2, 2)),
+                dma((3, 2)),
+                dma((2,)),
+                dma((3, 2)),
+                dma((SPOTS, 2)),
+                dma((2, 2)),
+                dma((2,)),
                 dma((SPOTS,)),
                 dma((SPOTS,)),
                 dma((n_help,)),

time: 54.5 us -> 52.3 us (0.960)
  Pallas kernels: 51 us -> 49 us
    pallas_call x1, Pallas kernels: 51 us -> 49 us  [on_device(): pl.pallas_call(functools.partial(kernel, n_pts, n_help), out_shape=(out,...]
where the time goes in v2:
time: 52.3 us; the launch traced here: 52.1 us
  Pallas kernels  49 us (94%)
  local copies, waits for them, and re-layouts  1.86 us (4%)
  between operations  1.3 us (2%)
    pallas_call x1, Pallas kernels, on_device(): pl.pallas_call(functools.partial(kernel, n_pts, n_help), out_shape=(out,...  49 us
    unnamed x6, local copies, waits for them, and re-layouts  1.86 us

profile of v2, /device:TPU:7, one launch (start us, length us, event | category | flops | bytes accessed | tf_op | source)
XLA Modules:
  0.0 52.1 jit_solution(15595935638204334700)
XLA Ops:
  1.3 49.0 %sinkhorn.1 = (f32[2,128]{1,0:T(2,128)}, f32[2,128]{1,0:T(2,128)}) custom-call(bf16[256,256]{1,0:T(8,128)(2,1)} %src_hbm.1, bf16[256,256]{1,0:T(8,128)(2,1)} %dst_hbm.1, f32[2,128]{1,0:T(2,128)} %bitcast.5, f32[2,128]{1,0:T(2,128)} %bitcast.6, f32[2,128]{1,0:T(2,128)} %bitcast.7, s32[1,24]{1,0:T(1,128)} %lists.1, s32[1]{0:T(128)S(6)} %copy.11.counts), custom_call_target="tpu_custom_call" | custom-call | tf_op jit(solution)/shard_map/sinkhorn/pallas_call | solution.py:521
  50.2 0.0 copy-start.1
  50.3 0.7 %copy-done.1 = f32[2,128]{1,0:T(2,128)S(1)} copy-done((f32[2,128]{1,0:T(2,128)S(1)}, f32[2,128]{1,0:T(2,128)}, u32[]{:S(2)}) %copy-start.1) | copy-done | bytes 1048
  50.9 0.0 copy-start
  50.9 0.6 %copy.12 = f32[256]{0:T(256)} copy(f32[256]{0:T(256)S(1)} %bitcast.9) | data formatting | bytes 2048
  51.5 0.1 copy-done
  51.5 0.6 %copy.13 = f32[256]{0:T(256)} copy(f32[256]{0:T(256)S(1)} %bitcast.8) | data formatting | bytes 2048
Async XLA Ops:
  50.2 0.7 %copy-start.1 = (f32[2,128]{1,0:T(2,128)S(1)}, f32[2,128]{1,0:T(2,128)}, u32[]{:S(2)}) copy-start(f32[2,128]{1,0:T(2,128)} %get-tuple-element.4) | copy-start | bytes 3076
  50.9 0.6 %copy-start = (f32[2,128]{1,0:T(2,128)S(1)}, f32[2,128]{1,0:T(2,128)}, u32[]{:S(2)}) copy-start(f32[2,128]{1,0:T(2,128)} %get-tuple-element.5) | copy-start | bytes 3076

commit v3 on v2

--- a/solution.py
+++ b/solution.py
@@ -48,13 +48,17 @@
     n_help,
     src_hbm,
     dst_hbm,
+    src_lw_hbm,
+    dst_lw_hbm,
+    init_g_hbm,
+    lists_hbm,
+    counts_hbm,
+    out,
     src_lw,
     dst_lw,
     init_g,
     lists,
     counts,
-    out_f,
-    out_g,
     xs,
     ys,
     vin,
@@ -63,8 +67,12 @@
     dots,
     peak,
     total,
+    cpeak,
+    ctotal,
+    push,
+    lift,
     bvec,
-    acol,
+    flast,
     lsend,
     lrecv,
     gsend,
@@ -130,6 +138,20 @@
 
     get_dst = pltpu.make_async_copy(dst_hbm, ys.at[REACH], local_sem.at[0])
     get_src = pltpu.make_async_copy(src_hbm, xs.at[h], local_sem.at[1])
+    get_small = [
+        pltpu.make_async_copy(a, b, local_sem.at[2 + n])
+        for n, (a, b) in enumerate(
+            [
+                (lists_hbm, lists),
+                (counts_hbm, counts),
+                (dst_lw_hbm, dst_lw),
+                (init_g_hbm, init_g),
+                (src_lw_hbm, src_lw),
+            ]
+        )
+    ]
+    for get in get_small:
+        get.start()
     get_dst.start()
     get_src.start()
 
@@ -230,8 +252,8 @@
             for k in range(SPOTS):
                 grecv[k, d + WIDE] = jnp.full(grecv.shape[2:], NEG, F32)
 
-    lane = lax.broadcasted_iota(jnp.int32, (8, 128), 1)
-    sub = lax.broadcasted_iota(jnp.int32, (8, 128), 0)
+    for get in get_small:
+        get.wait()
     listed = lists[...]
     width = listed.shape[1]
     slot = lax.broadcasted_iota(jnp.int32, (8, width), 1)
@@ -298,21 +320,17 @@
                 xs[r], ys[k], (((1,), (1,)), ((), ())), preferred_element_type=F32
             )
             inner = inner * SCALE
-            dots[k, 2 * r] = inner[0:half]
-            dots[k, 2 * r + 1] = inner[half:]
-
-    def first(c):
-        return lax.select(c < 2, REACH + c * side, REACH + 10 - 4 * c)
+            for j in range(2):
+                for q in range(2):
+                    dots[2 * k + j, 2 * r + q] = inner[half * q : half * q + half, 128 * j : 128 * j + 128]
+
+    soon = [h, helper(1), helper(n_help - 1)]
 
     def one_first(c, carry):
-        tiles(first(c), [helper(j) for j in (0, 1, 3)])
+        tiles(lax.select(c < 2, REACH + c * side, REACH + 10 - 4 * c), soon)
         return carry
 
-    def one_second(c, carry):
-        tiles(first(c), [helper(2)])
-        return carry
-
-    def one_third(c, carry):
+    def one_later(c, carry):
         d = lax.select(c < 2, side - 2 + 4 * c, -3 * side)
         k = REACH + d
 
@@ -321,18 +339,19 @@
             for q in range(2):
                 y_came(k, q).wait_recv()
 
-        tiles(k, range(n_help))
+        tiles(k, soon)
         return carry
 
     with jax.named_scope("tiles1"):
         lax.fori_loop(0, 4, one_first, 0)
+    with jax.named_scope("tiles2"):
+        lax.fori_loop(0, 3, one_later, 0)
     with jax.named_scope("xlast"):
         x_came(2, 0).wait_recv()
         x_came(2, 1).wait_recv()
-    with jax.named_scope("tiles2"):
-        lax.fori_loop(0, 4, one_second, 0)
     with jax.named_scope("tiles3"):
-        lax.fori_loop(0, 3, one_third, 0)
+        for k in range(SPOTS):
+            tiles(k, [helper(2)])
 
     with jax.named_scope("vec"):
         for j in range(1, n_help):
@@ -342,82 +361,122 @@
     for k in range(SPOTS):
         bvec[k] = vin[k, 0:2, :]
 
-    diagonal = lane - sub
-
-    def row_sweep():
-        def one(rh, carry):
-            r = rh // 2
-            push = []
+    def fold(parts):
+        top = tree(jnp.maximum, parts)
+        return top + log2(tree(jnp.add, [jnp.exp2(v - top) for v in parts]))
+
+    def f_copy(it, j, r):
+        return remote(
+            lsend.at[it, r],
+            lrecv.at[it, j, r],
+            f_send.at[it, j, r],
+            f_recv.at[it, j, r],
+            {"help": helper(j)},
+        )
+
+    lanes = 2 * SPOTS
+
+    def row_sweep(it):
+        def mask(r, carry):
             for k in range(SPOTS):
                 on = yin[r, k : k + 1, :] > 0.5
                 for j in range(2):
-                    row = jnp.where(on, bvec[k, j : j + 1, :], NEG)
-                    push.append(jnp.broadcast_to(row, (8, 128)))
-            found = jnp.zeros((8, 128), F32)
-            for g in range(16):
-                t = [
-                    dots[k, rh, 8 * g : 8 * g + 8, 128 * j : 128 * j + 128] + push[2 * k + j]
-                    for k in range(SPOTS)
-                    for j in range(2)
-                ]
-                top = tree(jnp.maximum, t)
-                s = tree(jnp.add, [jnp.exp2(v - top) for v in t])
-                most = jnp.max(top, axis=1, keepdims=True)
-                whole = jnp.sum(s * jnp.exp2(top - most), axis=1, keepdims=True)
-                found = jnp.where(diagonal == 8 * g, most + log2(whole), found)
-            lsend[pl.ds(rh, 1), :] = jnp.sum(found, axis=0, keepdims=True)
+                    push[r, 2 * k + j : 2 * k + j + 1, :] = jnp.where(on, bvec[k, j : j + 1, :], NEG)
             return carry
 
-        lax.fori_loop(0, 2 * n_help, one, 0)
-
-    def column_sweep():
-        def one(rh, carry):
-            row = jnp.broadcast_to(acol[pl.ds(rh, 1), :], (8, 128))
-            lift = [
-                jnp.broadcast_to(
-                    jnp.sum(jnp.where(diagonal == 8 * g, row, 0.0), axis=1, keepdims=True),
-                    (8, 128),
-                )
+        lax.fori_loop(0, n_help, mask, 0)
+
+        def load(r, n):
+            t = [
+                dots[c, 2 * r + n // 16, 8 * (n % 16) : 8 * (n % 16) + 8, :]
+                + jnp.broadcast_to(push[r, c : c + 1, :], (8, 128))
+                for c in range(lanes)
+            ]
+            return t, tree(jnp.maximum, t)
+
+        def close(r):
+            for q in range(2):
+                top = peak[2 * r + q].T
+                most = jnp.max(top, axis=0, keepdims=True)
+                s = total[2 * r + q].T * jnp.exp2(top - most)
+                lsend[it, r, q : q + 1, :] = most + log2(jnp.sum(s, axis=0, keepdims=True))
+
+        def send(r):
+            for j in range(1, n_help):
+                f_copy(it, j, r).start()
+
+        def one(r, carry):
+            before = jnp.maximum(r - 1, 0)
+            close(before)
+            t, top = load(r, 0)
+            for n in range(32):
+                later = load(r, n + 1) if n < 31 else None
+                at = slice(8 * (n % 16), 8 * (n % 16) + 8)
+                peak[2 * r + n // 16, at, :] = top
+                total[2 * r + n // 16, at, :] = tree(jnp.add, [jnp.exp2(v - top) for v in t])
+                if later:
+                    t, top = later
+
+            @pl.when(r > 0)
+            def _():
+                send(before)
+
+            return carry
+
+        with jax.named_scope("rmain"):
+            lax.fori_loop(0, n_help, one, 0)
+        with jax.named_scope("rclose"):
+            close(n_help - 1)
+        send(n_help - 1)
+
+    def column_sweep(it):
+        def load(r, n):
+            q, c = n // lanes, n % lanes
+            u = [
+                dots[c, 2 * r + q, 8 * g : 8 * g + 8, :] + lift[q, 8 * g : 8 * g + 8, :]
                 for g in range(16)
             ]
-            for k in range(SPOTS):
-                for j in range(2):
-                    u = [
-                        dots[k, rh, 8 * g : 8 * g + 8, 128 * j : 128 * j + 128] + lift[g]
-                        for g in range(16)
-                    ]
-                    top = tree(jnp.maximum, u)
-                    peak[2 * k + j, rh] = top
-                    total[2 * k + j, rh] = tree(jnp.add, [jnp.exp2(v - top) for v in u])
+            return u, tree(jnp.maximum, u)
+
+        def one(r, carry):
+            for j in range(1, n_help):
+                f_copy(it, j, r).wait_recv()
+            force = -fold([lsend[it, r]] + [lrecv[it, j, r] for j in range(1, n_help)])
+            if it == 1:
+                flast[r] = force
+            force = force + yin[r, 8:10, :]
+            for q in range(2):
+                lift[q] = jnp.broadcast_to(force[q : q + 1, :], (128, 128)).T
+            u, top = load(r, 0)
+            for n in range(2 * lanes):
+                later = load(r, n + 1) if n + 1 < 2 * lanes else None
+                q, c = n // lanes, n % lanes
+                cpeak[c, 2 * r + q] = top
+                ctotal[c, 2 * r + q] = tree(jnp.add, [jnp.exp2(v - top) for v in u])
+                if later:
+                    u, top = later
             return carry
 
-        lax.fori_loop(0, 2 * n_help, one, 0)
-
-        def close(k, carry):
+        with jax.named_scope("cmain"):
+            lax.fori_loop(0, n_help, one, 0)
+
+        def close(k):
             for j in range(2):
                 tops = [
-                    jnp.where(yin[rh // 2, pl.ds(k, 1), :] > 0.5, peak[2 * k + j, rh], NEG)
+                    jnp.where(yin[rh // 2, k : k + 1, :] > 0.5, cpeak[2 * k + j, rh], NEG)
                     for rh in range(2 * n_help)
                 ]
                 top = tree(jnp.maximum, tops)
                 most = jnp.max(top, axis=0, keepdims=True)
                 s = tree(
                     jnp.add,
-                    [total[2 * k + j, rh] * jnp.exp2(tops[rh] - most) for rh in range(2 * n_help)],
+                    [ctotal[2 * k + j, rh] * jnp.exp2(tops[rh] - most) for rh in range(2 * n_help)],
                 )
-                gsend[k, j : j + 1, :] = most + log2(jnp.sum(s, axis=0, keepdims=True))
-            return carry
-
-        lax.fori_loop(0, SPOTS, close, 0)
-
-    def fold(parts):
-        top = tree(jnp.maximum, parts)
-        return top + log2(tree(jnp.add, [jnp.exp2(v - top) for v in parts]))
-
-    def f_copy(it, j):
-        return remote(
-            lsend.at[it], lrecv.at[it, j], f_send.at[it, j], f_recv.at[it, j], {"help": helper(j)}
-        )
+                gsend[it, k, j : j + 1, :] = most + log2(jnp.sum(s, axis=0, keepdims=True))
+
+        with jax.named_scope("cclose"):
+            for k in range(SPOTS):
+                close(k)
 
     def g_copy(d):
         low, count = max(0, d), SPOTS - abs(d)
@@ -438,30 +497,15 @@
             {"pts": p + d},
         )
 
-    lsend_all, gsend_all = lsend, gsend
     for it in range(2):
-        lsend, gsend = lsend_all.at[it], gsend_all.at[it]
         with jax.named_scope('rows'):
-            row_sweep()
-        lsend, gsend = lsend_all, gsend_all
-        for j in range(1, n_help):
-            f_copy(it, j).start()
-        with jax.named_scope('fwait'):
-            for j in range(1, n_help):
-                f_copy(it, j).wait_recv()
-        force = -fold([lsend[it]] + [lrecv[it, j] for j in range(1, n_help)])
-        for r in range(n_help):
-            acol[2 * r : 2 * r + 2, :] = force[2 * r : 2 * r + 2, :] + yin[r, 8:10, :]
+            row_sweep(it)
+        with jax.named_scope('cols'):
+            column_sweep(it)
         if it == 1:
-            lrecv[1, 0] = force
-            out_f[0:1, :] = lrecv[1, 0, pl.ds(2 * h, 1), :] * (1.0 / SCALE) + src_half[0:1, 0:128]
-            out_f[1:2, :] = (
-                lrecv[1, 0, pl.ds(2 * h + 1, 1), :] * (1.0 / SCALE) + src_half[0:1, 128:256]
-            )
-        lsend, gsend = lsend_all.at[it], gsend_all.at[it]
-        with jax.named_scope('cols'):
-            column_sweep()
-        lsend, gsend = lsend_all, gsend_all
+            pot = flast[h] * (1.0 / SCALE)
+            out[0:1, :] = pot[0:1, :] + src_half[0:1, 0:128]
+            out[1:2, :] = pot[1:2, :] + src_half[0:1, 128:256]
         if it == 0:
             for d in wide:
                 when_there(d, lambda d=d: g_copy(d).start())
@@ -481,13 +525,14 @@
                 for d in near:
                     when_there(d, lambda d=d: e_copy(-d).wait_recv())
             pot = -fold([glast[k] for k in range(SPOTS)]) * (1.0 / SCALE)
-            out_g[0:1, :] = pot[0:1, :] + dst_half[0:1, 0:128]
-            out_g[1:2, :] = pot[1:2, :] + dst_half[0:1, 128:256]
+            out[2:3, :] = pot[0:1, :] + dst_half[0:1, 0:128]
+            out[3:4, :] = pot[1:2, :] + dst_half[0:1, 128:256]
 
     for j in range(1, n_help):
         row_copy(j).wait_send()
         for it in range(2):
-            f_copy(it, j).wait_send()
+            for r in range(n_help):
+                f_copy(it, j, r).wait_send()
     for way in range(2):
         x_on(way).wait_send()
         for q in range(2):
@@ -517,37 +562,40 @@
         vmem = pl.BlockSpec(memory_space=pltpu.VMEM)
         dma = pltpu.SemaphoreType.DMA
         bf16 = jnp.bfloat16
-        out = jax.ShapeDtypeStruct((2, 128), F32)
-        f, g = pl.pallas_call(
+        raw = pl.pallas_call(
             functools.partial(kernel, n_pts, n_help),
-            out_shape=(out, out),
+            out_shape=jax.ShapeDtypeStruct((4, 128), F32),
             in_specs=[
-                pl.BlockSpec(memory_space=pl.ANY),
-                pl.BlockSpec(memory_space=pl.ANY),
-                vmem,
-                vmem,
-                vmem,
-                vmem,
-                pl.BlockSpec(memory_space=pltpu.SMEM),
-            ],
-            out_specs=(vmem, vmem),
+                pl.BlockSpec(memory_space=pltpu.HBM),
+            ]
+            * 7,
+            out_specs=vmem,
             scratch_shapes=[
+                pltpu.VMEM((2, 128), F32),
+                pltpu.VMEM((2, 128), F32),
+                pltpu.VMEM((2, 128), F32),
+                pltpu.VMEM(pair_lists.shape, jnp.int32),
+                pltpu.SMEM((1,), jnp.int32),
                 pltpu.VMEM((n_help, BLOCK, dim), bf16),
                 pltpu.VMEM((SPOTS, BLOCK, dim), bf16),
                 pltpu.VMEM((SPOTS, 4, 128), F32),
                 pltpu.VMEM((n_help, 16, 128), F32),
                 pltpu.VMEM((n_help, 16, 128), F32),
-                pltpu.VMEM((SPOTS, 2 * n_help, 128, BLOCK), F32),
+                pltpu.VMEM((2 * SPOTS, 2 * n_help, 128, 128), F32),
+                pltpu.VMEM((2 * n_help, 128, 128), F32),
+                pltpu.VMEM((2 * n_help, 128, 128), F32),
                 pltpu.VMEM((2 * SPOTS, 2 * n_help, 8, 128), F32),
                 pltpu.VMEM((2 * SPOTS, 2 * n_help, 8, 128), F32),
+                pltpu.VMEM((n_help, 2 * SPOTS, 128), F32),
+                pltpu.VMEM((2, 128, 128), F32),
                 pltpu.VMEM((SPOTS, 2, 128), F32),
-                pltpu.VMEM((2 * n_help, 128), F32),
-                pltpu.VMEM((2, 2 * n_help, 128), F32),
-                pltpu.VMEM((2, n_help, 2 * n_help, 128), F32),
+                pltpu.VMEM((n_help, 2, 128), F32),
+                pltpu.VMEM((2, n_help, 2, 128), F32),
+                pltpu.VMEM((2, n_help, n_help, 2, 128), F32),
                 pltpu.VMEM((2, SPOTS, 2, 128), F32),
                 pltpu.VMEM((SPOTS, 2 * WIDE + 1, 2, 128), F32),
                 pltpu.VMEM((SPOTS, 2, 128), F32),
-                dma((2,)),
+                dma((7,)),
                 dma((2, 2)),
                 dma((3, 2)),
                 dma((2,)),
@@ -559,25 +607,19 @@
                 dma((SPOTS,)),
                 dma((n_help,)),
                 dma((n_help,)),
-                dma((2, n_help)),
-                dma((2, n_help)),
+                dma((2, n_help, n_help)),
+                dma((2, n_help, n_help)),
                 dma((2 * WIDE + 1,)),
                 dma((2 * WIDE + 1,)),
                 dma((SPOTS,)),
                 dma((SPOTS,)),
             ],
-            compiler_params=pltpu.CompilerParams(collective_id=0, has_side_effects=True),
+            compiler_params=pltpu.CompilerParams(collective_id=0, has_side_effects=True, vmem_limit_bytes=24 << 20),
             name="sinkhorn",
         )(
-            src_points,
-            dst_points,
-            src_logw.reshape(2, 128),
-            dst_logw.reshape(2, 128),
-            init_g.reshape(2, 128),
-            pair_lists,
-            pair_counts,
-        )
-        return f.reshape(-1), g.reshape(-1)
+            *(pltpu.with_memory_space_constraint(v, pltpu.HBM) for v in (src_points, dst_points, src_logw.reshape(2, 128), dst_logw.reshape(2, 128), init_g.reshape(2, 128), pair_lists)), pair_counts,
+        )
+        return raw[0:2].reshape(-1), raw[2:4].reshape(-1)
 
     rows = P(("pts", "help"))
     blocks = P(("pts", "help"), None)

time: 52.3 us -> 45.2 us (0.86)
  Pallas kernels: 49 us -> 43.2 us
  local copies, waits for them, and re-layouts: 1.86 us -> 0.57 us
    pallas_call x1, Pallas kernels: 49 us -> 43.2 us  [on_device(): pl.pallas_call(functools.partial(kernel, n_pts, n_help), out_shape=jax.Sh...]
    unnamed x6 -> x0, local copies, waits for them, and re-layouts: 1.86 us -> none
    reshape x0 -> x1, local copies, waits for them, and re-layouts: none -> 0.57 us  [on_device(): return (raw[0:2].reshape(-1), raw[2:4].reshape(-1))]
where the time goes in v3:
time: 45.2 us; the launch traced here: 45 us
  Pallas kernels  43.2 us (96%)
  between operations  1.29 us (3%)
  local copies, waits for them, and re-layouts  0.57 us (1%)
    pallas_call x1, Pallas kernels, on_device(): pl.pallas_call(functools.partial(kernel, n_pts, n_help), out_shape=jax.Sh...  43.2 us

profile of v3, /device:TPU:7, one launch (start us, length us, event | category | flops | bytes accessed | tf_op | source)
XLA Modules:
  0.0 45.0 jit_solution(1061649871729885337)
XLA Ops:
  1.3 43.2 %sinkhorn.1 = f32[4,128]{1,0:T(4,128)S(1)} custom-call(bf16[256,256]{1,0:T(8,128)(2,1)} %src_hbm.1, bf16[256,256]{1,0:T(8,128)(2,1)} %dst_hbm.1, f32[2,128]{1,0:T(2,128)} %bitcast.7, f32[2,128]{1,0:T(2,128)} %bitcast.8, f32[2,128]{1,0:T(2,128)} %bitcast.9, s32[1,24]{1,0:T(1,128)} %lists_hbm.1, s32[1]{0:T(128)S(6)} %copy.9.counts_hbm), custom_call_target="tpu_custom_call" | custom-call | tf_op jit(solution)/shard_map/sinkhorn/pallas_call | solution.py:565
  44.5 0.6 %slice_bitcast_fusion = (f32[256]{0:T(256)}, f32[256]{0:T(256)}) fusion(f32[4,128]{1,0:T(4,128)S(1)} %sinkhorn.1), kind=kLoop, calls=%fused_computation | loop fusion | bytes 4096 | tf_op jit(solution)/shard_map/reshape | solution.py:622

commit v4 on v3

--- a/solution.py
+++ b/solution.py
@@ -15,6 +15,8 @@
 LOG2E = 1.0 / math.log(2.0)
 SCALE = 4.0 * LOG2E
 NEG = -1e30
+FROM_VMEM = True
+SEND_AT = 8
 MESH = pl.DeviceIdType.MESH
 F32 = jnp.float32
 
@@ -54,9 +56,7 @@
     lists_hbm,
     counts_hbm,
     out,
-    src_lw,
-    dst_lw,
-    init_g,
+    vals,
     lists,
     counts,
     xs,
@@ -79,23 +79,12 @@
     grecv,
     glast,
     local_sem,
-    x_send,
+    sent,
     x_recv,
-    x_pass,
-    y_send,
     y_recv,
-    y_pass,
-    y_far,
-    vec_send,
-    vec_recv,
-    row_send,
-    row_recv,
-    f_send,
     f_recv,
-    g_send,
     g_recv,
-    e_send,
-    e_recv,
+    came,
 ):
     p = lax.axis_index("pts")
     h = lax.axis_index("help")
@@ -137,23 +126,15 @@
         )
 
     get_dst = pltpu.make_async_copy(dst_hbm, ys.at[REACH], local_sem.at[0])
-    get_src = pltpu.make_async_copy(src_hbm, xs.at[h], local_sem.at[1])
-    get_small = [
-        pltpu.make_async_copy(a, b, local_sem.at[2 + n])
-        for n, (a, b) in enumerate(
-            [
-                (lists_hbm, lists),
-                (counts_hbm, counts),
-                (dst_lw_hbm, dst_lw),
-                (init_g_hbm, init_g),
-                (src_lw_hbm, src_lw),
-            ]
-        )
+    get_src = pltpu.make_async_copy(src_hbm, xs.at[h], local_sem.at[4])
+    get_vals = [
+        pltpu.make_async_copy(a, vals.at[n], local_sem.at[3])
+        for n, a in enumerate([dst_lw_hbm, init_g_hbm, src_lw_hbm])
     ]
-    for get in get_small:
+    get_lists = pltpu.make_async_copy(lists_hbm, lists, local_sem.at[1])
+    get_counts = pltpu.make_async_copy(counts_hbm, counts, local_sem.at[2])
+    for get in [get_dst, get_src, get_lists, get_counts, *get_vals]:
         get.start()
-    get_dst.start()
-    get_src.start()
 
     with jax.named_scope("barrier"):
         pl.semaphore_wait(
@@ -166,67 +147,70 @@
 
     ahead, behind = {"help": helper(1)}, {"help": helper(n_help - 1)}
 
+    own_x, own_y = (xs.at[h], ys.at[REACH]) if FROM_VMEM else (src_hbm, dst_hbm)
+
     def x_own(way, q):
         return remote(
-            src_hbm.at[parts[q]],
+            own_x.at[parts[q]],
             xs.at[h, parts[q]],
-            x_send.at[way, q],
-            x_recv.at[way, q],
+            sent.at[0],
+            x_recv.at[way if q == way else 2],
             (ahead, behind)[way],
         )
 
     def x_on(way):
         r = helper(n_help - 1 if way == 0 else 1)
         here = xs.at[r, parts[way]]
-        return remote(here, here, x_pass.at[way], x_recv.at[2, way], (ahead, behind)[way])
+        return remote(here, here, sent.at[0], x_recv.at[3], (ahead, behind)[way])
 
     def y_own(way, q):
         d = (2, -2)[way]
         return remote(
-            dst_hbm.at[parts[q]],
+            own_y.at[parts[q]],
             ys.at[REACH - d, parts[q]],
-            y_send.at[way, q],
-            y_recv.at[REACH - d, q],
+            sent.at[1],
+            y_recv.at[2 * way + q],
             {"pts": p + d},
         )
 
     def y_side():
-        return remote(
-            dst_hbm, ys.at[REACH - side], y_send.at[2, 0], y_recv.at[REACH - side, 0], {"pts": p + side}
-        )
+        return remote(own_y, ys.at[REACH - side], sent.at[1], y_recv.at[4], {"pts": p + side})
 
     def y_on(way, q):
         d = (-2, 2)[way]
-        k = REACH + d - side
         return remote(
             ys.at[REACH + d, parts[q]],
-            ys.at[k, parts[q]],
-            y_pass.at[way, q],
-            y_recv.at[k, q],
+            ys.at[REACH + d - side, parts[q]],
+            sent.at[1],
+            y_recv.at[5 + way],
             {"pts": p + side},
         )
 
     def y_over(q):
-        k = REACH + 3 * side
         return remote(
             ys.at[REACH + 2 * side, parts[q]],
-            ys.at[k, parts[q]],
-            y_far.at[q],
-            y_recv.at[k, q],
+            ys.at[REACH + 3 * side, parts[q]],
+            sent.at[1],
+            y_recv.at[7],
             {"pts": p - side},
         )
 
-    def y_came(k, q):
-        return remote(
-            dst_hbm.at[parts[q]], ys.at[k, parts[q]], y_far.at[0], y_recv.at[k, q], {"pts": p + side}
-        )
-
-    def x_came(way, q):
-        r = helper((n_help - 1, 1, 2)[way])
-        return remote(
-            src_hbm.at[parts[q]], xs.at[r, parts[q]], x_pass.at[0], x_recv.at[way, q], ahead
-        )
-
+    def arrive(ref, sem):
+        remote(ref, ref, sent.at[0], sem, ahead).wait_recv()
+
+    def leave(ref, sem):
+        remote(ref, ref, sem, x_recv.at[0], ahead).wait_send()
+
+    def by_count(count, most, do):
+        for c in range(1, most + 1):
+            pl.when(count == c)(lambda c=c: do(c))
+
+    lefts, rights = jnp.minimum(p, WIDE), jnp.minimum(n_pts - 1 - p, WIDE)
+    nears = jnp.minimum(p, REACH) + jnp.minimum(n_pts - 1 - p, REACH)
+
+    if FROM_VMEM:
+        get_dst.wait()
+        get_src.wait()
     x_own(0, 0).start()
     x_own(1, 1).start()
     when_there(2, lambda: y_own(0, 0).start())
@@ -249,11 +233,12 @@
 
         @pl.when(jnp.logical_not(there(d)))
         def _():
-            for k in range(SPOTS):
-                grecv[k, d + WIDE] = jnp.full(grecv.shape[2:], NEG, F32)
-
-    for get in get_small:
+            grecv[d + WIDE] = jnp.full(grecv.shape[1:], NEG, F32)
+
+    for get in [get_lists, get_counts]:
         get.wait()
+    remote(vals, vals, local_sem.at[3], x_recv.at[0], ahead).wait_send()
+    dst_lw, init_g, src_lw = vals.at[0], vals.at[1], vals.at[2]
     listed = lists[...]
     width = listed.shape[1]
     slot = lax.broadcasted_iota(jnp.int32, (8, width), 1)
@@ -267,7 +252,8 @@
             jnp.concatenate([src_lw[...] * LOG2E] * 4, axis=0), (8, 128)
         )
 
-    get_dst.wait()
+    if not FROM_VMEM:
+        get_dst.wait()
     dst_half = half_norms(ys[REACH])
     vin[REACH, 0:1, :] = dst_lw[0:1, :] * LOG2E + SCALE * (init_g[0:1, :] - dst_half[0:1, 0:128])
     vin[REACH, 1:2, :] = dst_lw[1:2, :] * LOG2E + SCALE * (init_g[1:2, :] - dst_half[0:1, 128:256])
@@ -275,12 +261,12 @@
 
     def vec_copy(d):
         return remote(
-            vin.at[REACH], vin.at[REACH - d], vec_send.at[d + REACH], vec_recv.at[REACH - d], {"pts": p + d}
+            vin.at[REACH], vin.at[REACH - d], sent.at[2], came.at[0], {"pts": p + d}
         )
 
     def row_copy(j):
         return remote(
-            yout.at[helper(j)], yin.at[h], row_send.at[j], row_recv.at[j], {"help": helper(j)}
+            yout.at[helper(j)], yin.at[h], sent.at[3], came.at[1], {"help": helper(j)}
         )
 
     steps = [1, -1, 2, -2, 3, -3]
@@ -289,20 +275,21 @@
     for d in steps:
         when_there(d, lambda d=d: vec_copy(d).start())
     yin[h] = yout[h]
-    get_src.wait()
+    if not FROM_VMEM:
+        get_src.wait()
     src_half = half_norms(xs[h])
 
     with jax.named_scope("relay"):
-        x_came(0, 0).wait_recv()
+        arrive(xs.at[0, parts[0]], x_recv.at[0])
         x_on(0).start()
-        x_came(1, 1).wait_recv()
+        arrive(xs.at[0, parts[0]], x_recv.at[1])
         x_on(1).start()
         for q in range(2):
             for way, d in enumerate((-2, 2)):
 
                 @pl.when(there(d))
                 def _(way=way, d=d, q=q):
-                    y_came(REACH + d, q).wait_recv()
+                    arrive(ys.at[0, parts[0]], y_recv.at[2 * way + q])
 
                     @pl.when((2 * side == d) & there(-side))
                     def _():
@@ -310,9 +297,8 @@
 
                     y_on(way, q).start()
 
-        x_came(0, 1).wait_recv()
-        x_came(1, 0).wait_recv()
-        remote(dst_hbm, ys.at[REACH + side], y_far.at[0], y_recv.at[REACH + side, 0], {"pts": p + side}).wait_recv()
+        arrive(xs.at[0], x_recv.at[2])
+        arrive(ys.at[0], y_recv.at[4])
 
     def tiles(k, rows):
         for r in rows:
@@ -336,8 +322,7 @@
 
         @pl.when(there(d))
         def _():
-            for q in range(2):
-                y_came(k, q).wait_recv()
+            arrive(ys.at[0], y_recv.at[5 + c])
 
         tiles(k, soon)
         return carry
@@ -347,17 +332,14 @@
     with jax.named_scope("tiles2"):
         lax.fori_loop(0, 3, one_later, 0)
     with jax.named_scope("xlast"):
-        x_came(2, 0).wait_recv()
-        x_came(2, 1).wait_recv()
+        arrive(xs.at[0], x_recv.at[3])
     with jax.named_scope("tiles3"):
         for k in range(SPOTS):
             tiles(k, [helper(2)])
 
     with jax.named_scope("vec"):
-        for j in range(1, n_help):
-            row_copy(j).wait_recv()
-        for d in steps:
-            when_there(d, lambda d=d: vec_copy(-d).wait_recv())
+        arrive(yin.at[0 : n_help - 1], came.at[1])
+        by_count(nears, 2 * REACH, lambda c: arrive(vin.at[0:c], came.at[0]))
     for k in range(SPOTS):
         bvec[k] = vin[k, 0:2, :]
 
@@ -368,9 +350,9 @@
     def f_copy(it, j, r):
         return remote(
             lsend.at[it, r],
-            lrecv.at[it, j, r],
-            f_send.at[it, j, r],
-            f_recv.at[it, j, r],
+            lrecv.at[it, r, j - 1],
+            sent.at[4],
+            f_recv.at[it, r],
             {"help": helper(j)},
         )
 
@@ -402,7 +384,7 @@
                 lsend[it, r, q : q + 1, :] = most + log2(jnp.sum(s, axis=0, keepdims=True))
 
         def send(r):
-            for j in range(1, n_help):
+            for j in (2, 1, 3):
                 f_copy(it, j, r).start()
 
         def one(r, carry):
@@ -416,10 +398,11 @@
                 total[2 * r + n // 16, at, :] = tree(jnp.add, [jnp.exp2(v - top) for v in t])
                 if later:
                     t, top = later
-
-            @pl.when(r > 0)
-            def _():
-                send(before)
+                if n == SEND_AT:
+
+                    @pl.when(r > 0)
+                    def _():
+                        send(before)
 
             return carry
 
@@ -439,9 +422,8 @@
             return u, tree(jnp.maximum, u)
 
         def one(r, carry):
-            for j in range(1, n_help):
-                f_copy(it, j, r).wait_recv()
-            force = -fold([lsend[it, r]] + [lrecv[it, j, r] for j in range(1, n_help)])
+            arrive(lrecv.at[it, r], f_recv.at[it, r])
+            force = -fold([lsend[it, r]] + [lrecv[it, r, j] for j in range(n_help - 1)])
             if it == 1:
                 flast[r] = force
             force = force + yin[r, 8:10, :]
@@ -482,19 +464,19 @@
         low, count = max(0, d), SPOTS - abs(d)
         return remote(
             gsend.at[0, pl.ds(low, count)],
-            grecv.at[pl.ds(low, count), WIDE - d],
-            g_send.at[d + WIDE],
-            g_recv.at[WIDE - d],
+            grecv.at[WIDE - d, pl.ds(low, count)],
+            sent.at[6 if d < 0 else 7],
+            g_recv.at[1 if d < 0 else 0],
             {"pts": p + d},
         )
 
+    def g_bytes(c):
+        most, spots = ((1, 6), (11, 1), (3, 5), (3, 6), (4, 5), (3, 7))[c - 1]
+        return grecv.at[0:most, 0:spots]
+
     def e_copy(d):
         return remote(
-            gsend.at[1, d + REACH],
-            glast.at[REACH - d],
-            e_send.at[d + REACH],
-            e_recv.at[REACH - d],
-            {"pts": p + d},
+            gsend.at[1, d + REACH], glast.at[REACH - d], sent.at[5], came.at[2], {"pts": p + d}
         )
 
     for it in range(2):
@@ -507,51 +489,37 @@
             out[0:1, :] = pot[0:1, :] + src_half[0:1, 0:128]
             out[1:2, :] = pot[1:2, :] + src_half[0:1, 128:256]
         if it == 0:
-            for d in wide:
+            for d in sorted(wide, key=lambda d: -abs(d)):
                 when_there(d, lambda d=d: g_copy(d).start())
+            grecv[WIDE] = gsend[0]
+            with jax.named_scope('gwait'):
+                by_count(lefts, WIDE, lambda c: arrive(g_bytes(c), g_recv.at[0]))
+                by_count(rights, WIDE, lambda c: arrive(g_bytes(c), g_recv.at[1]))
             for k in range(SPOTS):
-                grecv[k, WIDE] = gsend[0, k]
-            with jax.named_scope('gwait'):
-                for d in wide:
-                    when_there(d, lambda d=d: g_copy(-d).wait_recv())
-            for k in range(SPOTS):
-                came = [grecv[REACH - e, k + REACH + e] for e in range(-REACH, REACH + 1)]
-                bvec[k] = vin[k, 2:4, :] - fold(came)
+                got = [grecv[k + REACH + e, REACH - e] for e in range(-REACH, REACH + 1)]
+                bvec[k] = vin[k, 2:4, :] - fold(got)
         else:
-            for d in near:
+            for d in sorted(near, key=lambda d: -abs(d)):
                 when_there(d, lambda d=d: e_copy(d).start())
             glast[REACH] = gsend[1, REACH]
             with jax.named_scope('ewait'):
-                for d in near:
-                    when_there(d, lambda d=d: e_copy(-d).wait_recv())
+                by_count(nears, 2 * REACH, lambda c: arrive(glast.at[0:c], came.at[2]))
             pot = -fold([glast[k] for k in range(SPOTS)]) * (1.0 / SCALE)
             out[2:3, :] = pot[0:1, :] + dst_half[0:1, 0:128]
             out[3:4, :] = pot[1:2, :] + dst_half[0:1, 128:256]
 
-    for j in range(1, n_help):
-        row_copy(j).wait_send()
-        for it in range(2):
-            for r in range(n_help):
-                f_copy(it, j, r).wait_send()
-    for way in range(2):
-        x_on(way).wait_send()
-        for q in range(2):
-            x_own(way, q).wait_send()
-    y_side().wait_send()
-    for q in range(2):
-        for way, d in enumerate((2, -2)):
-            when_there(d, lambda way=way, q=q: y_own(way, q).wait_send())
-            when_there(-d, lambda way=way, q=q: y_on(way, q).wait_send())
-        pl.when(there(2 * side) & there(-side))(lambda q=q: y_over(q).wait_send())
-    for d in near:
-
-        @pl.when(there(d))
-        def _(d=d):
-            vec_copy(d).wait_send()
-            e_copy(d).wait_send()
-
-    for d in wide:
-        when_there(d, lambda d=d: g_copy(d).wait_send())
+    def one_if(d):
+        return there(d).astype(jnp.int32)
+
+    blocks = 1 + 2 * one_if(2) + 2 * one_if(-2) + (there(2 * side) & there(-side)).astype(jnp.int32)
+    leave(xs.at[0 : n_help - 1], sent.at[0])
+    by_count(blocks, 6, lambda c: leave(ys.at[0:c], sent.at[1]))
+    by_count(nears, 2 * REACH, lambda c: leave(vin.at[0:c], sent.at[2]))
+    leave(yin.at[0 : n_help - 1], sent.at[3])
+    leave(lrecv, sent.at[4])
+    by_count(nears, 2 * REACH, lambda c: leave(glast.at[0:c], sent.at[5]))
+    by_count(lefts, WIDE, lambda c: leave(g_bytes(c), sent.at[6]))
+    by_count(rights, WIDE, lambda c: leave(g_bytes(c), sent.at[7]))
 
 
 def solution(mesh):
@@ -571,9 +539,7 @@
             * 7,
             out_specs=vmem,
             scratch_shapes=[
-                pltpu.VMEM((2, 128), F32),
-                pltpu.VMEM((2, 128), F32),
-                pltpu.VMEM((2, 128), F32),
+                pltpu.VMEM((3, 2, 128), F32),
                 pltpu.VMEM(pair_lists.shape, jnp.int32),
                 pltpu.SMEM((1,), jnp.int32),
                 pltpu.VMEM((n_help, BLOCK, dim), bf16),
@@ -591,28 +557,17 @@
                 pltpu.VMEM((SPOTS, 2, 128), F32),
                 pltpu.VMEM((n_help, 2, 128), F32),
                 pltpu.VMEM((2, n_help, 2, 128), F32),
-                pltpu.VMEM((2, n_help, n_help, 2, 128), F32),
+                pltpu.VMEM((2, n_help, n_help - 1, 2, 128), F32),
                 pltpu.VMEM((2, SPOTS, 2, 128), F32),
-                pltpu.VMEM((SPOTS, 2 * WIDE + 1, 2, 128), F32),
+                pltpu.VMEM((2 * WIDE + 1, SPOTS, 2, 128), F32),
                 pltpu.VMEM((SPOTS, 2, 128), F32),
-                dma((7,)),
-                dma((2, 2)),
-                dma((3, 2)),
+                dma((5,)),
+                dma((8,)),
+                dma((4,)),
+                dma((8,)),
+                dma((2, n_help)),
                 dma((2,)),
-                dma((3, 2)),
-                dma((SPOTS, 2)),
-                dma((2, 2)),
-                dma((2,)),
-                dma((SPOTS,)),
-                dma((SPOTS,)),
-                dma((n_help,)),
-                dma((n_help,)),
-                dma((2, n_help, n_help)),
-                dma((2, n_help, n_help)),
-                dma((2 * WIDE + 1,)),
-                dma((2 * WIDE + 1,)),
-                dma((SPOTS,)),
-                dma((SPOTS,)),
+                dma((3,)),
             ],
             compiler_params=pltpu.CompilerParams(collective_id=0, has_side_effects=True, vmem_limit_bytes=24 << 20),
             name="sinkhorn",

time: 45.2 us -> 42.8 us (0.947)
  Pallas kernels: 43.2 us -> 40.8 us
    pallas_call x1, Pallas kernels: 43.2 us -> 40.8 us  [on_device(): pl.pallas_call(functools.partial(kernel, n_pts, n_help), out_shape=jax.Sh...]
where the time goes in v4:
time: 42.8 us; the launch traced here: 42.6 us
  Pallas kernels  40.8 us (95%)
  between operations  1.29 us (3%)
  local copies, waits for them, and re-layouts  0.57 us (1%)
    pallas_call x1, Pallas kernels, on_device(): pl.pallas_call(functools.partial(kernel, n_pts, n_help), out_shape=jax.Sh...  40.8 us

profile of v4, /device:TPU:7, one launch (start us, length us, event | category | flops | bytes accessed | tf_op | source)
XLA Modules:
  0.0 42.6 jit_solution(2611880004986663253)
XLA Ops:
  1.3 40.8 %sinkhorn.1 = f32[4,128]{1,0:T(4,128)S(1)} custom-call(bf16[256,256]{1,0:T(8,128)(2,1)} %src_hbm.1, bf16[256,256]{1,0:T(8,128)(2,1)} %dst_hbm.1, f32[2,128]{1,0:T(2,128)} %bitcast.7, f32[2,128]{1,0:T(2,128)} %bitcast.8, f32[2,128]{1,0:T(2,128)} %bitcast.9, s32[1,24]{1,0:T(1,128)} %lists_hbm.1, s32[1]{0:T(128)S(6)} %copy.9.counts_hbm), custom_call_target="tpu_custom_call" | custom-call | tf_op jit(solution)/shard_map/sinkhorn/pallas_call | solution.py:533
  42.1 0.6 %slice_bitcast_fusion = (f32[256]{0:T(256)}, f32[256]{0:T(256)}) fusion(f32[4,128]{1,0:T(4,128)S(1)} %sinkhorn.1), kind=kLoop, calls=%fused_computation | loop fusion | bytes 4096 | tf_op jit(solution)/shard_map/reshape | solution.py:577

commit v5 on v4

--- a/solution.py
+++ b/solution.py
@@ -16,7 +16,9 @@
 SCALE = 4.0 * LOG2E
 NEG = -1e30
 FROM_VMEM = True
-SEND_AT = 8
+SEND_AT = 15
+CLOSE_AT = 17
+LATE_LATER = True
 MESH = pl.DeviceIdType.MESH
 F32 = jnp.float32
 
@@ -149,40 +151,41 @@
 
     own_x, own_y = (xs.at[h], ys.at[REACH]) if FROM_VMEM else (src_hbm, dst_hbm)
 
+    quarter = half // 2
+
     def x_own(way, q):
-        return remote(
-            own_x.at[parts[q]],
-            xs.at[h, parts[q]],
+        rows = pl.ds(half * way + quarter * q, quarter) if q < 2 else parts[1 - way]
+        return remote(
+            own_x.at[rows],
+            xs.at[h, rows],
             sent.at[0],
-            x_recv.at[way if q == way else 2],
+            x_recv.at[2 * way + q if q < 2 else 4],
             (ahead, behind)[way],
         )
 
-    def x_on(way):
+    def x_on(way, q):
         r = helper(n_help - 1 if way == 0 else 1)
-        here = xs.at[r, parts[way]]
-        return remote(here, here, sent.at[0], x_recv.at[3], (ahead, behind)[way])
-
-    def y_own(way, q):
-        d = (2, -2)[way]
+        here = xs.at[r, pl.ds(half * way + quarter * q, quarter)]
+        return remote(here, here, sent.at[0], x_recv.at[5], (ahead, behind)[way])
+
+    def y_own(d, q):
         return remote(
             own_y.at[parts[q]],
             ys.at[REACH - d, parts[q]],
             sent.at[1],
-            y_recv.at[2 * way + q],
+            y_recv.at[lax.div(2 - d, 2) + q],
             {"pts": p + d},
         )
 
     def y_side():
         return remote(own_y, ys.at[REACH - side], sent.at[1], y_recv.at[4], {"pts": p + side})
 
-    def y_on(way, q):
-        d = (-2, 2)[way]
+    def y_on(d, q):
         return remote(
             ys.at[REACH + d, parts[q]],
             ys.at[REACH + d - side, parts[q]],
             sent.at[1],
-            y_recv.at[5 + way],
+            y_recv.at[5 + lax.div(d + 2, 4)],
             {"pts": p + side},
         )
 
@@ -211,15 +214,17 @@
     if FROM_VMEM:
         get_dst.wait()
         get_src.wait()
-    x_own(0, 0).start()
-    x_own(1, 1).start()
-    when_there(2, lambda: y_own(0, 0).start())
-    when_there(-2, lambda: y_own(1, 0).start())
-    x_own(0, 1).start()
-    x_own(1, 0).start()
-    when_there(2, lambda: y_own(0, 1).start())
-    when_there(-2, lambda: y_own(1, 1).start())
+    early, late = -2 * side, 2 * side
+    for q in range(2):
+        x_own(0, q).start()
+        x_own(1, q).start()
+        when_there(early, lambda q=q: y_own(early, q).start())
     y_side().start()
+    x_own(0, 2).start()
+    x_own(1, 2).start()
+    if not LATE_LATER:
+        for q in range(2):
+            when_there(late, lambda q=q: y_own(late, q).start())
 
     for d in near:
 
@@ -274,30 +279,35 @@
         row_copy(j).start()
     for d in steps:
         when_there(d, lambda d=d: vec_copy(d).start())
+    if LATE_LATER:
+        for q in range(2):
+            when_there(late, lambda q=q: y_own(late, q).start())
     yin[h] = yout[h]
     if not FROM_VMEM:
         get_src.wait()
     src_half = half_norms(xs[h])
 
     with jax.named_scope("relay"):
-        arrive(xs.at[0, parts[0]], x_recv.at[0])
-        x_on(0).start()
-        arrive(xs.at[0, parts[0]], x_recv.at[1])
-        x_on(1).start()
-        for q in range(2):
-            for way, d in enumerate((-2, 2)):
-
-                @pl.when(there(d))
-                def _(way=way, d=d, q=q):
-                    arrive(ys.at[0, parts[0]], y_recv.at[2 * way + q])
-
-                    @pl.when((2 * side == d) & there(-side))
-                    def _():
-                        y_over(q).start()
-
-                    y_on(way, q).start()
-
-        arrive(xs.at[0], x_recv.at[2])
+        def pass_x(q):
+            for way in range(2):
+                arrive(xs.at[0, pl.ds(0, quarter)], x_recv.at[2 * way + q])
+                x_on(way, q).start()
+
+        def pass_y(d, q, over):
+            @pl.when(there(d))
+            def _():
+                arrive(ys.at[0, parts[0]], y_recv.at[lax.div(d + 2, 2) + q])
+                if over:
+                    when_there(-side, lambda: y_over(q).start())
+                y_on(d, q).start()
+
+        pass_x(0)
+        pass_x(1)
+        pass_y(2 * side, 0, True)
+        pass_y(2 * side, 1, True)
+        pass_y(-2 * side, 0, False)
+        pass_y(-2 * side, 1, False)
+        arrive(xs.at[0], x_recv.at[4])
         arrive(ys.at[0], y_recv.at[4])
 
     def tiles(k, rows):
@@ -329,13 +339,24 @@
 
     with jax.named_scope("tiles1"):
         lax.fori_loop(0, 4, one_first, 0)
-    with jax.named_scope("tiles2"):
+    def from_opposite():
+        arrive(xs.at[0], x_recv.at[5])
+
+    @pl.when(side > 0)
+    def _():
         lax.fori_loop(0, 3, one_later, 0)
-    with jax.named_scope("xlast"):
-        arrive(xs.at[0], x_recv.at[3])
-    with jax.named_scope("tiles3"):
+        from_opposite()
         for k in range(SPOTS):
             tiles(k, [helper(2)])
+
+    @pl.when(side < 0)
+    def _():
+        lax.fori_loop(0, 2, one_later, 0)
+        from_opposite()
+        for k in range(SPOTS - 1):
+            tiles(k, [helper(2)])
+        when_there(REACH, lambda: arrive(ys.at[0], y_recv.at[7]))
+        tiles(SPOTS - 1, [*soon, helper(2)])
 
     with jax.named_scope("vec"):
         arrive(yin.at[0 : n_help - 1], came.at[1])
@@ -346,6 +367,27 @@
     def fold(parts):
         top = tree(jnp.maximum, parts)
         return top + log2(tree(jnp.add, [jnp.exp2(v - top) for v in parts]))
+
+    def g_copy(d):
+        low, count = max(0, d), SPOTS - abs(d)
+        return remote(
+            gsend.at[0, pl.ds(low, count)],
+            grecv.at[WIDE - d, pl.ds(low, count)],
+            sent.at[6 if d < 0 else 7],
+            g_recv.at[1 if d < 0 else 0],
+            {"pts": p + d},
+        )
+
+    def g_bytes(c):
+        most, spots = ((1, 6), (11, 1), (3, 5), (3, 6), (4, 5), (3, 7))[c - 1]
+        return grecv.at[0:most, 0:spots]
+
+    def e_copy(d):
+        return remote(
+            gsend.at[1, d + REACH], glast.at[REACH - d], sent.at[5], came.at[2], {"pts": p + d}
+        )
+
+    rows_of = 2 * n_help
 
     def f_copy(it, j, r):
         return remote(
@@ -376,12 +418,11 @@
             ]
             return t, tree(jnp.maximum, t)
 
-        def close(r):
-            for q in range(2):
-                top = peak[2 * r + q].T
-                most = jnp.max(top, axis=0, keepdims=True)
-                s = total[2 * r + q].T * jnp.exp2(top - most)
-                lsend[it, r, q : q + 1, :] = most + log2(jnp.sum(s, axis=0, keepdims=True))
+        def close(r, q):
+            top = peak[2 * r + q].T
+            most = jnp.max(top, axis=0, keepdims=True)
+            s = total[2 * r + q].T * jnp.exp2(top - most)
+            lsend[it, r, q : q + 1, :] = most + log2(jnp.sum(s, axis=0, keepdims=True))
 
         def send(r):
             for j in (2, 1, 3):
@@ -389,7 +430,7 @@
 
         def one(r, carry):
             before = jnp.maximum(r - 1, 0)
-            close(before)
+            close(before, 1)
             t, top = load(r, 0)
             for n in range(32):
                 later = load(r, n + 1) if n < 31 else None
@@ -404,24 +445,19 @@
                     def _():
                         send(before)
 
+                if n == CLOSE_AT:
+                    close(r, 0)
+
             return carry
 
         with jax.named_scope("rmain"):
             lax.fori_loop(0, n_help, one, 0)
         with jax.named_scope("rclose"):
-            close(n_help - 1)
+            close(n_help - 1, 1)
         send(n_help - 1)
 
     def column_sweep(it):
-        def load(r, n):
-            q, c = n // lanes, n % lanes
-            u = [
-                dots[c, 2 * r + q, 8 * g : 8 * g + 8, :] + lift[q, 8 * g : 8 * g + 8, :]
-                for g in range(16)
-            ]
-            return u, tree(jnp.maximum, u)
-
-        def one(r, carry):
+        def begin(r):
             arrive(lrecv.at[it, r], f_recv.at[it, r])
             force = -fold([lsend[it, r]] + [lrecv[it, r, j] for j in range(n_help - 1)])
             if it == 1:
@@ -429,55 +465,58 @@
             force = force + yin[r, 8:10, :]
             for q in range(2):
                 lift[q] = jnp.broadcast_to(force[q : q + 1, :], (128, 128)).T
-            u, top = load(r, 0)
-            for n in range(2 * lanes):
-                later = load(r, n + 1) if n + 1 < 2 * lanes else None
-                q, c = n // lanes, n % lanes
+
+        def chunks(r, columns):
+            def load(q, c):
+                u = [
+                    dots[c, 2 * r + q, 8 * g : 8 * g + 8, :] + lift[q, 8 * g : 8 * g + 8, :]
+                    for g in range(16)
+                ]
+                return u, tree(jnp.maximum, u)
+
+            order = [(q, c) for q in range(2) for c in columns]
+            u, top = load(*order[0])
+            for (q, c), following in zip(order, [*order[1:], None]):
+                later = None if following is None else load(*following)
                 cpeak[c, 2 * r + q] = top
                 ctotal[c, 2 * r + q] = tree(jnp.add, [jnp.exp2(v - top) for v in u])
                 if later:
                     u, top = later
-            return carry
-
-        with jax.named_scope("cmain"):
-            lax.fori_loop(0, n_help, one, 0)
 
         def close(k):
             for j in range(2):
                 tops = [
                     jnp.where(yin[rh // 2, k : k + 1, :] > 0.5, cpeak[2 * k + j, rh], NEG)
-                    for rh in range(2 * n_help)
+                    for rh in range(rows_of)
                 ]
                 top = tree(jnp.maximum, tops)
                 most = jnp.max(top, axis=0, keepdims=True)
                 s = tree(
                     jnp.add,
-                    [ctotal[2 * k + j, rh] * jnp.exp2(tops[rh] - most) for rh in range(2 * n_help)],
+                    [ctotal[2 * k + j, rh] * jnp.exp2(tops[rh] - most) for rh in range(rows_of)],
                 )
                 gsend[it, k, j : j + 1, :] = most + log2(jnp.sum(s, axis=0, keepdims=True))
 
-        with jax.named_scope("cclose"):
-            for k in range(SPOTS):
+        def one(r, carry):
+            begin(r)
+            chunks(r, range(lanes))
+            return carry
+
+        with jax.named_scope("cmain"):
+            lax.fori_loop(0, n_help - 1, one, 0)
+        begin(n_help - 1)
+        far = WIDE if it == 0 else REACH
+        for spots, reaches in (
+            ((6, 0), (far,)),
+            ((5, 1), (far - 1,)),
+            ((4, 2, 3), range(far - 2, 0, -1)),
+        ):
+            chunks(n_help - 1, [2 * k + j for k in spots for j in range(2)])
+            for k in spots:
                 close(k)
-
-    def g_copy(d):
-        low, count = max(0, d), SPOTS - abs(d)
-        return remote(
-            gsend.at[0, pl.ds(low, count)],
-            grecv.at[WIDE - d, pl.ds(low, count)],
-            sent.at[6 if d < 0 else 7],
-            g_recv.at[1 if d < 0 else 0],
-            {"pts": p + d},
-        )
-
-    def g_bytes(c):
-        most, spots = ((1, 6), (11, 1), (3, 5), (3, 6), (4, 5), (3, 7))[c - 1]
-        return grecv.at[0:most, 0:spots]
-
-    def e_copy(d):
-        return remote(
-            gsend.at[1, d + REACH], glast.at[REACH - d], sent.at[5], came.at[2], {"pts": p + d}
-        )
+            for d in reaches:
+                for way in (d, -d):
+                    when_there(way, lambda d=way: (e_copy if it else g_copy)(d).start())
 
     for it in range(2):
         with jax.named_scope('rows'):
@@ -489,8 +528,6 @@
             out[0:1, :] = pot[0:1, :] + src_half[0:1, 0:128]
             out[1:2, :] = pot[1:2, :] + src_half[0:1, 128:256]
         if it == 0:
-            for d in sorted(wide, key=lambda d: -abs(d)):
-                when_there(d, lambda d=d: g_copy(d).start())
             grecv[WIDE] = gsend[0]
             with jax.named_scope('gwait'):
                 by_count(lefts, WIDE, lambda c: arrive(g_bytes(c), g_recv.at[0]))
@@ -499,8 +536,6 @@
                 got = [grecv[k + REACH + e, REACH - e] for e in range(-REACH, REACH + 1)]
                 bvec[k] = vin[k, 2:4, :] - fold(got)
         else:
-            for d in sorted(near, key=lambda d: -abs(d)):
-                when_there(d, lambda d=d: e_copy(d).start())
             glast[REACH] = gsend[1, REACH]
             with jax.named_scope('ewait'):
                 by_count(nears, 2 * REACH, lambda c: arrive(glast.at[0:c], came.at[2]))
@@ -563,7 +598,7 @@
                 pltpu.VMEM((SPOTS, 2, 128), F32),
                 dma((5,)),
                 dma((8,)),
-                dma((4,)),
+                dma((6,)),
                 dma((8,)),
                 dma((2, n_help)),
                 dma((2,)),

time: 42.8 us -> 42.5 us (level)
  no operation moved by 1% of the time
where the time goes in v5:
time: 42.5 us; the launch traced here: 42.3 us
  Pallas kernels  40.4 us (95%)
  between operations  1.29 us (3%)
  local copies, waits for them, and re-layouts  0.57 us (1%)
    pallas_call x1, Pallas kernels, on_device(): pl.pallas_call(functools.partial(kernel, n_pts, n_help), out_shape=jax.Sh...  40.4 us

profile of v5, /device:TPU:7, one launch (start us, length us, event | category | flops | bytes accessed | tf_op | source)
XLA Modules:
  0.0 42.3 jit_solution(12506644617650967510)
XLA Ops:
  1.3 40.4 %sinkhorn.1 = f32[4,128]{1,0:T(4,128)S(1)} custom-call(bf16[256,256]{1,0:T(8,128)(2,1)} %src_hbm.1, bf16[256,256]{1,0:T(8,128)(2,1)} %dst_hbm.1, f32[2,128]{1,0:T(2,128)} %bitcast.7, f32[2,128]{1,0:T(2,128)} %bitcast.8, f32[2,128]{1,0:T(2,128)} %bitcast.9, s32[1,24]{1,0:T(1,128)} %lists_hbm.1, s32[1]{0:T(128)S(6)} %copy.9.counts_hbm), custom_call_target="tpu_custom_call" | custom-call | tf_op jit(solution)/shard_map/sinkhorn/pallas_call | solution.py:568
  41.7 0.6 %slice_bitcast_fusion = (f32[256]{0:T(256)}, f32[256]{0:T(256)}) fusion(f32[4,128]{1,0:T(4,128)S(1)} %sinkhorn.1), kind=kLoop, calls=%fused_computation | loop fusion | bytes 4096 | tf_op jit(solution)/shard_map/reshape | solution.py:612

commit v6 on v5

--- a/solution.py
+++ b/solution.py
@@ -287,29 +287,6 @@
         get_src.wait()
     src_half = half_norms(xs[h])
 
-    with jax.named_scope("relay"):
-        def pass_x(q):
-            for way in range(2):
-                arrive(xs.at[0, pl.ds(0, quarter)], x_recv.at[2 * way + q])
-                x_on(way, q).start()
-
-        def pass_y(d, q, over):
-            @pl.when(there(d))
-            def _():
-                arrive(ys.at[0, parts[0]], y_recv.at[lax.div(d + 2, 2) + q])
-                if over:
-                    when_there(-side, lambda: y_over(q).start())
-                y_on(d, q).start()
-
-        pass_x(0)
-        pass_x(1)
-        pass_y(2 * side, 0, True)
-        pass_y(2 * side, 1, True)
-        pass_y(-2 * side, 0, False)
-        pass_y(-2 * side, 1, False)
-        arrive(xs.at[0], x_recv.at[4])
-        arrive(ys.at[0], y_recv.at[4])
-
     def tiles(k, rows):
         for r in rows:
             inner = lax.dot_general(
@@ -320,38 +297,60 @@
                 for q in range(2):
                     dots[2 * k + j, 2 * r + q] = inner[half * q : half * q + half, 128 * j : 128 * j + 128]
 
+    tiles(REACH, [h])
+    arrive(ys.at[0], y_recv.at[4])
+    tiles(REACH + side, [h])
+
+    with jax.named_scope("relay"):
+        def pass_x(q):
+            for way in range(2):
+                arrive(xs.at[0, pl.ds(0, quarter)], x_recv.at[2 * way + q])
+                x_on(way, q).start()
+
+        def pass_y(d, q, over):
+            @pl.when(there(d))
+            def _():
+                arrive(ys.at[0, parts[0]], y_recv.at[lax.div(d + 2, 2) + q])
+                if over:
+                    when_there(-side, lambda: y_over(q).start())
+                y_on(d, q).start()
+
+        pass_x(0)
+        pass_x(1)
+        pass_y(2 * side, 0, True)
+        pass_y(2 * side, 1, True)
+        pass_y(-2 * side, 0, False)
+        pass_y(-2 * side, 1, False)
+        arrive(xs.at[0], x_recv.at[4])
+
     soon = [h, helper(1), helper(n_help - 1)]
 
-    def one_first(c, carry):
-        tiles(lax.select(c < 2, REACH + c * side, REACH + 10 - 4 * c), soon)
-        return carry
-
-    def one_later(c, carry):
-        d = lax.select(c < 2, side - 2 + 4 * c, -3 * side)
-        k = REACH + d
-
-        @pl.when(there(d))
-        def _():
-            arrive(ys.at[0], y_recv.at[5 + c])
-
-        tiles(k, soon)
-        return carry
-
     with jax.named_scope("tiles1"):
-        lax.fori_loop(0, 4, one_first, 0)
+        for k in (REACH, REACH + side):
+            tiles(k, soon[1:])
+        for k in (REACH + 2, REACH - 2):
+            tiles(k, soon)
+
+    def later(count):
+        slots = [(c, d) for c, d in enumerate((side - 2, side + 2, -3 * side))][:count]
+        for c, d in slots:
+            when_there(d, lambda c=c: arrive(ys.at[0], y_recv.at[5 + c]))
+        for c, d in slots:
+            tiles(REACH + d, soon)
+
     def from_opposite():
         arrive(xs.at[0], x_recv.at[5])
 
     @pl.when(side > 0)
     def _():
-        lax.fori_loop(0, 3, one_later, 0)
+        later(3)
         from_opposite()
         for k in range(SPOTS):
             tiles(k, [helper(2)])
 
     @pl.when(side < 0)
     def _():
-        lax.fori_loop(0, 2, one_later, 0)
+        later(2)
         from_opposite()
         for k in range(SPOTS - 1):
             tiles(k, [helper(2)])

time: 42.5 us -> 42.2 us (level)
  no operation moved by 1% of the time
where the time goes in v6:
time: 42.2 us; the launch traced here: 42 us
  Pallas kernels  40.2 us (95%)
  between operations  1.29 us (3%)
  local copies, waits for them, and re-layouts  0.57 us (1%)
    pallas_call x1, Pallas kernels, on_device(): pl.pallas_call(functools.partial(kernel, n_pts, n_help), out_shape=jax.Sh...  40.2 us

profile of v6, /device:TPU:7, one launch (start us, length us, event | category | flops | bytes accessed | tf_op | source)
XLA Modules:
  0.0 42.0 jit_solution(1388856095648610511)
XLA Ops:
  1.3 40.2 %sinkhorn.1 = f32[4,128]{1,0:T(4,128)S(1)} custom-call(bf16[256,256]{1,0:T(8,128)(2,1)} %src_hbm.1, bf16[256,256]{1,0:T(8,128)(2,1)} %dst_hbm.1, f32[2,128]{1,0:T(2,128)} %bitcast.7, f32[2,128]{1,0:T(2,128)} %bitcast.8, f32[2,128]{1,0:T(2,128)} %bitcast.9, s32[1,24]{1,0:T(1,128)} %lists_hbm.1, s32[1]{0:T(128)S(6)} %copy.9.counts_hbm), custom_call_target="tpu_custom_call" | custom-call | tf_op jit(solution)/shard_map/sinkhorn/pallas_call | solution.py:567
  41.5 0.6 %slice_bitcast_fusion = (f32[256]{0:T(256)}, f32[256]{0:T(256)}) fusion(f32[4,128]{1,0:T(4,128)S(1)} %sinkhorn.1), kind=kLoop, calls=%fused_computation | loop fusion | bytes 4096 | tf_op jit(solution)/shard_map/reshape | solution.py:611
